TPU v7x, 32 devices: a whole 2x2x4 slice. The times are simulated.
32 devices in a mesh: tm: 8 (over y, x, core), group: 4 (over z).
Axes of the slice: x: 2, y: 2, z: 4, core: 2. Of those that a mesh axis runs over, the one named last changes fastest.
Arguments:
- propagators: float32 [8, 384, 384], P('tm'), may hold values from -1 to 1, as said below
- perturbation: float32 [8, 384, 384], P('tm', 'group'), as said below
Outputs:
- gradient: float32 [384, 384], P('tm')
Inputs may be any that keep to these rules, and one draw needn't show every extreme that they name: `propagators`: each slice's matrix is orthogonal. `perturbation`: each slice's matrix is symmetric.
All inputs are finite; a program needn't handle non-finite values.
Results may differ from a plain program's by a relative error of at most 0.00028.
Values sent between devices are 32-bit elements; how exact they have to be, the bound alone decides.
No kernel may reach another device: no remote copies, remote signals or barrier semaphores. Data moves between devices by JAX's collectives and lax.ppermute only.
A program may use at most 128 MiB of HBM per device.

v0:
```python
import jax
import jax.numpy as jnp
from jax import lax
from jax.sharding import PartitionSpec as P


def carried_in(part, axis, combine, identity):
    place = lax.axis_index(axis)
    gathered = lax.all_gather(part, axis)
    state = jnp.zeros_like(part) + jnp.asarray(identity, part.dtype)

    def one(lap, state):
        return combine(state, lax.dynamic_index_in_dim(gathered, lap, 0, False))

    return lax.fori_loop(0, place, one, state)


def times_high(left, right):
    return jnp.dot(left, right, precision=lax.Precision.HIGHEST, preferred_element_type=jnp.float32)


def compose(earlier, later):
    return times_high(later, earlier)


def body(propagators, perturbation):
    slice_count = propagators.shape[0]
    order_dim = propagators.shape[1]
    block_rows = perturbation.shape[1]
    identity = jnp.eye(order_dim, dtype=jnp.float32)
    local_prefixes = [identity]
    device_total = times_high(propagators[slice_count - 1], local_prefixes[-1])
    before = carried_in(device_total, "tm", compose, identity)
    first_block = lax.axis_index("group") * block_rows
    prefix_rows = lax.dynamic_slice_in_dim(before, first_block, block_rows, 0)
    pulled = times_high(perturbation[0], before)
    conjugated = times_high(prefix_rows.T, pulled)
    row_sums = lax.psum_scatter(conjugated, "tm", scatter_dimension=0, tiled=True)
    return lax.psum(row_sums, "group")


def solution(mesh):
    in_specs = (P("tm", None, None), P("tm", "group", None))
    out_specs = P("tm", None)
    return jax.shard_map(body, mesh=mesh, in_specs=in_specs, out_specs=out_specs, check_vma=False)
```

profile of v0, /device:TPU:0, one launch (start us, length us, event | category | flops | bytes accessed | tf_op | source)
XLA Modules:
  0.0 155.6 jit_solution(5823865246684013293)
XLA Ops:
  6.5 0.0 copy-start
  6.5 0.0 all-gather.3.cloned.1.call-start
  6.5 1.1 copy-done
  7.6 1.6 %convolution_bitcast_fusion = f32[384,384]{0,1:T(8,128)} fusion(f32[1,384,384]{2,1,0:T(8,128)S(1)} %copy-done), kind=kOutput, calls=%fused_computation.4 | convolution fusion | flops 679772160 | bytes 1179648 | tf_op jit(solution)/shard_map/dot_general | solution.py:19
  9.2 0.0 all-gather.3.cloned.1.call-update
  9.2 0.0 reduce-scatter.2.cloned.1.call-start
  9.3 41.5 %all-gather.3.cloned.1.call-done = f32[3072,384]{0,1:T(8,128)} async-done(((f32[384,384]{0,1:T(8,128)}), f32[3072,384]{0,1:T(8,128)}) %all-gather.3.cloned.1.call-update) | async-done | bytes 4718608 | tf_op jit(solution)/shard_map/all_gather | solution.py:9
  50.8 6.1 %copy.4 = f32[3072,384]{1,0:T(8,128)} copy(f32[3072,384]{0,1:T(8,128)} %all-gather.3.cloned.1.call-done) | data formatting | bytes 9437184 | tf_op jit(solution)/shard_map/while | solution.py:15
  56.9 0.0 copy-start.1
  56.9 0.9 copy-done.1
  57.8 1.1 fusion.8
  58.9 1.7 %fusion.10 = f32[384,384]{1,0:T(8,128)} fusion(f32[384,96]{1,0:T(8,128)S(1)} %fusion.8, f32[384,384]{1,0:T(8,128)S(1)} %get-tuple-element.28, s32[]{:T(128)S(6)} %select_n.7), kind=kOutput, calls=%fused_computation.11 | convolution fusion | flops 169869312 | bytes 933892 | tf_op jit(solution)/shard_map/dot_general | solution.py:19
  60.6 0.0 reduce-scatter.2.cloned.1.call-update
  60.6 0.0 all-reduce.2.cloned.1.call-start
  60.7 50.3 %reduce-scatter.2.cloned.1.call-done = f32[48,384]{1,0:T(8,128)} async-done(((f32[384,384]{1,0:T(8,128)}), f32[48,384]{1,0:T(8,128)}) %reduce-scatter.2.cloned.1.call-update) | async-done | bytes 73744 | tf_op jit(solution)/shard_map/reduce_scatter | solution.py:38
  111.0 0.0 all-reduce.2.cloned.1.call-update
  111.0 36.6 %all-reduce.2.cloned.1.call-done = f32[48,384]{1,0:T(8,128)} async-done(((f32[48,384]{1,0:T(8,128)}), f32[48,384]{1,0:T(8,128)}) %all-reduce.2.cloned.1.call-update) | async-done | bytes 73744 | tf_op jit(solution)/shard_map/psum | solution.py:39
  147.6 1.5 copy.14
  (2 shorter events, 0.0 us)
Async XLA Ops:
  6.5 1.1 copy-start
  6.5 44.3 %all-gather.3.cloned.1.call-start = ((), (), s32[]{:S(2)}) async-start(), calls=%async_computation.3 | async-start | bytes 5308416 | tf_op jit(solution)/shard_map/all_gather | solution.py:9
  9.2 101.7 %reduce-scatter.2.cloned.1.call-start = ((), (), s32[]{:S(2)}) async-start(), calls=%async_computation.1 | async-start | bytes 663552 | tf_op jit(solution)/shard_map/reduce_scatter | solution.py:38
  56.9 0.9 copy-start.1
  60.6 86.9 %all-reduce.2.cloned.1.call-start = ((), (), s32[]{:S(2)}) async-start(), calls=%async_computation.2 | async-start | bytes 147456 | tf_op jit(solution)/shard_map/psum | solution.py:39
Sparse Core Ops, SparseCore 0:
  9.4 41.4 all-gather.2
  60.7 50.1 reduce-scatter.1
  113.3 34.2 all-reduce.1
where the time goes:
time: 156 us
  waiting for transfers between devices  128 us (82%)
  between operations  13.1 us (8%)
  local copies, waits for them, and re-layouts  9.54 us (6%)
  matrix products  4.43 us (3%)
    reduce_scatter x1, waiting for transfers between devices, body(): lax.psum_scatter(conjugated, 'tm', scatter_dimension=0, tiled=True)  50.3 us
    all_gather x1, waiting for transfers between devices, carried_in(): gathered = lax.all_gather(part, axis)  41.5 us
    psum x1, waiting for transfers between devices, body(): return lax.psum(row_sums, 'group')  36.6 us
    while x1, local copies, waits for them, and re-layouts, carried_in(): return lax.fori_loop(0, place, one, state)  6.05 us
    dot_general x3, matrix products, times_high(): jnp.dot(left, right, precision=lax.Precision.HIGHEST, preferred_element_t...  4.43 us
    unnamed x5, local copies, waits for them, and re-layouts  3.49 us
  transfers between devices with their start and end apart: 3, of which 3 were waited for; matrix products, arithmetic and copies ran while one was open for 0% of the time, Pallas kernels for 0%

commit v1 on v0

v1 whole, which is shorter than its diff:
```python
import jax
import jax.numpy as jnp
from jax import lax
from jax.sharding import PartitionSpec as P


def times(left, right):
    return lax.dot_general(left, right, (((1,), (0,)), ((), ())), precision=lax.Precision.HIGH, preferred_element_type=jnp.float32)


def times_t(left, right):
    return lax.dot_general(left, right, (((1,), (1,)), ((), ())), precision=lax.Precision.HIGH, preferred_element_type=jnp.float32)


def t_times(left, right):
    return lax.dot_general(left, right, (((0,), (0,)), ((), ())), precision=lax.Precision.HIGH, preferred_element_type=jnp.float32)


def body(propagators, perturbation):
    devices = lax.axis_size("tm")
    planes = lax.axis_size("group")
    chips = devices // 2
    order_dim = propagators.shape[1]
    block_rows = perturbation.shape[1]
    out_rows = order_dim // devices
    place = lax.axis_index("tm")
    plane = lax.axis_index("group")
    chip, core = place // 2, place % 2
    partner = [(i, i ^ 1) for i in range(devices)]

    own = propagators[0]
    other = lax.ppermute(own, "tm", partner)
    even = jnp.where(core == 0, own, other)
    odd = jnp.where(core == 0, other, own)

    rows = perturbation[0]
    full = jnp.zeros((order_dim, order_dim), jnp.float32)
    full = lax.dynamic_update_slice_in_dim(full, rows, plane * block_rows, 0)
    for shift in range(1, planes):
        got = lax.ppermute(rows, "group", [(i, (i + shift) % planes) for i in range(planes)])
        full = lax.dynamic_update_slice_in_dim(full, got, (plane - shift) % planes * block_rows, 0)

    pair = lax.dot_general(even, odd, (((0,), (1,)), ((), ())), precision=lax.Precision.HIGH, preferred_element_type=jnp.float32)

    def half_of(whole):
        split = whole.reshape(chips, 2, out_rows, order_dim)
        return lax.dynamic_index_in_dim(split, core, 1, False)

    half = half_of(pair)
    halves = []
    for shift in range(1, chips):
        halves.append(lax.ppermute(half, "tm", [(i, i + 2 * shift) for i in range(devices - 2 * shift)]))

    full_other = lax.ppermute(full, "tm", partner)
    full_even = jnp.where(core == 0, full, full_other)
    full_odd = jnp.where(core == 0, full_other, full)
    total = full_even + t_times(even, times(full_odd, even))

    identity = jnp.eye(order_dim, dtype=jnp.float32)
    for shift in range(1, chips):
        mine = halves[shift - 1]
        theirs = lax.ppermute(mine, "tm", partner)
        low = jnp.where(core == 0, mine, theirs)
        high = jnp.where(core == 0, theirs, mine)
        whole = jnp.stack([low, high], 1).reshape(order_dim, order_dim)
        whole = jnp.where(chip >= shift, whole, identity)
        if shift < chips - 1:
            total = times_t(times(whole, total), whole)
        else:
            left = jnp.where(chip >= shift, mine, half_of(identity)).reshape(order_dim // 2, order_dim)
            terms = times_t(times(left, total), whole).reshape(chips, out_rows, order_dim)
    out = lax.dynamic_index_in_dim(terms, chip, 0, False)
    for shift in range(1, chips):
        block = lax.dynamic_index_in_dim(terms, (chip + shift) % chips, 0, False)
        out = out + lax.ppermute(block, "tm", [(i, (i + 2 * shift) % devices) for i in range(devices)])
    return out


def solution(mesh):
    in_specs = (P("tm", None, None), P("tm", "group", None))
    out_specs = P("tm", None)
    return jax.shard_map(body, mesh=mesh, in_specs=in_specs, out_specs=out_specs, check_vma=False)
```

time: 156 us -> 50.5 us (0.32)
  waiting for transfers between devices: 128 us -> 19.4 us
  starting transfers between devices: 0.09 us -> 21.2 us
  between operations: 13.1 us -> 0.41 us
  local copies, waits for them, and re-layouts: 9.54 us -> 1.23 us
  matrix products: 4.43 us -> 6.46 us
    reduce_scatter x1 -> x0, waiting for transfers between devices: 50.3 us -> none  [body(): lax.psum_scatter(conjugated, 'tm', scatter_dimension=0, tiled=True)]
    all_gather x1 -> x0, waiting for transfers between devices: 41.5 us -> none  [carried_in(): gathered = lax.all_gather(part, axis)]
    psum x1 -> x0, waiting for transfers between devices: 36.6 us -> none  [body(): return lax.psum(row_sums, 'group')]
    ppermute x0 -> x14, starting transfers between devices: none -> 21.2 us  [the longest x3 8.15 us: body(): lax.ppermute(half, 'tm', [(i, i + 2 * shift) for i in range(devices - 2 *...]
    ppermute x0 -> x14, waiting for transfers between devices: none -> 19.4 us  [the longest x3 8.14 us: body(): lax.ppermute(rows, 'group', [(i, (i + shift) % planes) for i in range(pla...]
    while x1 -> x0, local copies, waits for them, and re-layouts: 6.05 us -> none  [carried_in(): return lax.fori_loop(0, place, one, state)]
    unnamed x5 -> x4, local copies, waits for them, and re-layouts: 3.49 us -> 0.9 us
    dot_general x3 -> x9, matrix products: 4.43 us -> 6.46 us  [the longest x4 2.65 us: times(): lax.dot_general(left, right, (((1,), (0,)), ((), ())), precision=lax.Prec...]
  transfers between devices with their start and end apart: 3 -> 14, of which waited for: 3 -> 7; matrix products, arithmetic and copies ran while one was open for 0% -> 12% of each run, Pallas kernels for 0% -> 0%
where the time goes in v1:
time: 50.5 us; the launch traced here: 49.8 us
  starting transfers between devices  21.2 us (42%)
  waiting for transfers between devices  19.4 us (38%)
  matrix products  6.46 us (13%)
  local copies, waits for them, and re-layouts  1.23 us (2%)
  other arithmetic  1.13 us (2%)
    ppermute x3, starting transfers between devices, body(): lax.ppermute(half, 'tm', [(i, i + 2 * shift) for i in range(devices - 2 *...  8.15 us
    ppermute x3, waiting for transfers between devices, body(): lax.ppermute(rows, 'group', [(i, (i + shift) % planes) for i in range(pla...  8.14 us
    ppermute x3, waiting for transfers between devices, body(): lax.ppermute(half, 'tm', [(i, i + 2 * shift) for i in range(devices - 2 *...  7.74 us
    ppermute x3, starting transfers between devices, body(): lax.ppermute(rows, 'group', [(i, (i + shift) % planes) for i in range(pla...  6.5 us
    ppermute x3, starting transfers between devices, body(): lax.ppermute(block, 'tm', [(i, (i + 2 * shift) % devices) for i in range(...  5.45 us
    ppermute x3, waiting for transfers between devices, body(): lax.ppermute(block, 'tm', [(i, (i + 2 * shift) % devices) for i in range(...  3.47 us
    dot_general x4, matrix products, times(): lax.dot_general(left, right, (((1,), (0,)), ((), ())), precision=lax.Prec...  2.65 us
    dot_general x3, matrix products, times_t(): lax.dot_general(left, right, (((1,), (1,)), ((), ())), precision=lax.Prec...  1.94 us
  transfers between devices with their start and end apart: 14, of which 7 were waited for; matrix products, arithmetic and copies ran while one was open for 12% of the time, Pallas kernels for 0%

profile of v1, /device:TPU:0, one launch (start us, length us, event | category | flops | bytes accessed | tf_op | source)
XLA Modules:
  0.0 49.8 jit_solution(8344814574635432323)
XLA Ops:
  0.0 0.5 collective-permute-start
  0.5 2.6 %collective-permute-start.6 = (f32[96,384]{1,0:T(8,128)}, f32[96,384]{1,0:T(8,128)S(1)}, u32[]{:S(2)}, u32[]{:S(2)}) collective-permute-start(f32[96,384]{1,0:T(8,128)} %bitcast.72), channel_id=1, source_target_pairs={{0,1},{1,2},{2,3},{3,0},{4,5},{5,6},{6,7},{7,4},{8,9},{9,10},{10,1... | collective-permute-start | bytes 442376 | tf_op jit(solution)/shard_map/ppermute | solution.py:40
  3.1 2.6 %collective-permute-start.7 = (f32[96,384]{1,0:T(8,128)}, f32[96,384]{1,0:T(8,128)S(1)}, u32[]{:S(2)}, u32[]{:S(2)}) collective-permute-start(f32[96,384]{1,0:T(8,128)} %bitcast.73), channel_id=1, source_target_pairs={{0,2},{1,3},{2,0},{3,1},{4,6},{5,7},{6,4},{7,5},{8,10},{9,11},{10,... | collective-permute-start | bytes 442376 | tf_op jit(solution)/shard_map/ppermute | solution.py:40
  5.6 1.3 %collective-permute-start.8 = (f32[96,384]{1,0:T(8,128)}, f32[96,384]{1,0:T(8,128)S(1)}, u32[]{:S(2)}, u32[]{:S(2)}) collective-permute-start(f32[96,384]{1,0:T(8,128)} %bitcast.74), channel_id=1, source_target_pairs={{0,3},{1,0},{2,1},{3,2},{4,7},{5,4},{6,5},{7,6},{8,11},{9,8},{10,9... | collective-permute-start | bytes 442376 | tf_op jit(solution)/shard_map/ppermute | solution.py:40
  7.0 0.0 copy-start.1
  7.0 0.9 %copy-done.1 = f32[1,96,384]{2,1,0:T(8,128)S(1)} copy-done((f32[1,96,384]{2,1,0:T(8,128)S(1)}, f32[1,96,384]{2,1,0:T(8,128)}, u32[]{:S(2)}) %copy-start.1) | copy-done | bytes 147480
  7.9 0.0 copy-start
  8.0 2.0 %collective-permute-done.6 = f32[96,384]{1,0:T(8,128)S(1)} collective-permute-done((f32[96,384]{1,0:T(8,128)}, f32[96,384]{1,0:T(8,128)S(1)}, u32[]{:S(2)}, u32[]{:S(2)}) %collective-permute-start.6) | collective-permute-done | bytes 147488 | tf_op jit(solution)/shard_map/ppermute | solution.py:40
  10.1 6.1 %collective-permute-done.7 = f32[96,384]{1,0:T(8,128)S(1)} collective-permute-done((f32[96,384]{1,0:T(8,128)}, f32[96,384]{1,0:T(8,128)S(1)}, u32[]{:S(2)}, u32[]{:S(2)}) %collective-permute-start.7) | collective-permute-done | bytes 147488 | tf_op jit(solution)/shard_map/ppermute | solution.py:40
  16.2 0.0 collective-permute-done.8
  16.2 0.1 collective-permute-start.9
  16.3 0.0 collective-permute-done
  16.3 0.0 copy-done
  16.3 1.1 %fusion.7 = f32[384,384]{1,0:T(8,128)S(1)} fusion(f32[384,384]{1,0:T(8,128)S(1)} %collective-permute-done, pred[]{:T(512)S(6)} %eq.32, f32[1,384,384]{2,1,0:T(8,128)S(1)} %copy-done), kind=kOutput, calls=%fused_computation.16 | convolution fusion | flops 340033536 | bytes 1769473 | tf_op jit(solution)/shard_map/dot_general | solution.py:43
  17.5 3.4 %collective-permute-start.4 = (f32[4,48,384]{2,1,0:T(8,128)S(1)}, f32[4,48,384]{2,1,0:T(8,128)S(1)}, u32[]{:S(2)}, u32[]{:S(2)}) collective-permute-start(f32[4,48,384]{2,1,0:T(8,128)S(1)} %dynamic-slice_bitcast_fusion), channel_id=1, source_target_pairs={{0,8},{4,12},{8,16},{12,20},{16,24},{20,28},{1,9},{5,13},{9,17},{1... | collective-permute-start | bytes 884744 | tf_op jit(solution)/shard_map/ppermute | solution.py:52
  21.0 0.1 iota.89
  21.1 3.4 %collective-permute-start.2 = (f32[4,48,384]{2,1,0:T(8,128)S(1)}, f32[4,48,384]{2,1,0:T(8,128)S(1)}, u32[]{:S(2)}, u32[]{:S(2)}) collective-permute-start(f32[4,48,384]{2,1,0:T(8,128)S(1)} %dynamic-slice_bitcast_fusion), channel_id=1, source_target_pairs={{0,16},{4,20},{8,24},{12,28},{1,17},{5,21},{9,25},{13,29},{2,18},{... | collective-permute-start | bytes 884744 | tf_op jit(solution)/shard_map/ppermute | solution.py:52
  24.5 1.3 %collective-permute-start.1 = (f32[4,48,384]{2,1,0:T(8,128)S(1)}, f32[4,48,384]{2,1,0:T(8,128)S(1)}, u32[]{:S(2)}, u32[]{:S(2)}) collective-permute-start(f32[4,48,384]{2,1,0:T(8,128)S(1)} %dynamic-slice_bitcast_fusion), channel_id=1, source_target_pairs={{0,24},{4,28},{1,25},{5,29},{2,26},{6,30},{3,27},{7,31}} | collective-permute-start | bytes 884744 | tf_op jit(solution)/shard_map/ppermute | solution.py:52
  25.8 2.5 %collective-permute-done.4 = f32[4,48,384]{2,1,0:T(8,128)S(1)} collective-permute-done((f32[4,48,384]{2,1,0:T(8,128)S(1)}, f32[4,48,384]{2,1,0:T(8,128)S(1)}, u32[]{:S(2)}, u32[]{:S(2)}) %collective-permute-start.4) | collective-permute-done | bytes 294944 | tf_op jit(solution)/shard_map/ppermute | solution.py:52
  28.3 0.0 collective-permute-start.5
  28.3 0.0 collective-permute-done.9
  28.3 0.7 %fusion.4 = f32[384,384]{1,0:T(8,128)S(1)} fusion(f32[384,384]{1,0:T(8,128)S(1)} %collective-permute-done.9, f32[384,384]{1,0:T(8,128)S(1)} %constant_dynamic-update-slice_fusion, pred[]{:T(512)S(6)} %eq.32, f32[384,384]{1,0:T(8,128)S(1)} %collective-permute-done, f32[1,384,384]{2,1,0:T(8,128)S(1)} %copy-done), kind=kOutput, calls=%fused_computation.12 | convolution fusion | flops 340033536 | bytes 2949121 | tf_op jit(solution)/shard_map/dot_general | solution.py:8
  29.0 0.8 %fusion.14 = f32[384,384]{1,0:T(8,128)S(1)} fusion(f32[384,384]{1,0:T(8,128)S(1)} %fusion.4, f32[384,384]{1,0:T(8,128)S(1)} %collective-permute-done, pred[]{:T(512)S(6)} %eq.32, f32[1,384,384]{2,1,0:T(8,128)S(1)} %copy-done), kind=kOutput, calls=%fused_computation.33 | convolution fusion | flops 339886080 | bytes 2359297 | tf_op jit(solution)/shard_map/dot_general | solution.py:16
  29.8 5.3 %collective-permute-done.2 = f32[4,48,384]{2,1,0:T(8,128)S(1)} collective-permute-done((f32[4,48,384]{2,1,0:T(8,128)S(1)}, f32[4,48,384]{2,1,0:T(8,128)S(1)}, u32[]{:S(2)}, u32[]{:S(2)}) %collective-permute-start.2) | collective-permute-done | bytes 294944 | tf_op jit(solution)/shard_map/ppermute | solution.py:52
  35.1 0.0 collective-permute-start.3
  35.1 0.0 collective-permute-done.1
  35.1 0.5 collective-permute-start.10
  35.6 0.0 collective-permute-done.5
  35.8 0.7 %fusion.2 = f32[384,384]{1,0:T(8,128)S(1)} fusion(f32[384,384]{1,0:T(8,128)S(1)} %convert_select_fusion, f32[384,384]{1,0:T(8,128)S(1)} %fusion.14, f32[384,384]{1,0:T(8,128)S(1)} %constant_dynamic-update-slice_fusion, f32[384,384]{1,0:T(8,128)S(1)} %collective-permute-done.9, pred[]{:T(512)S(6)} %eq.32), kind=kOutput, calls=%fused_computation.10 | convolution fusion | flops 340033536 | bytes 2949121 | tf_op jit(solution)/shard_map/dot_general | solution.py:8
  36.5 0.7 %fusion.22 = f32[384,384]{1,0:T(8,128)S(1)} fusion(f32[384,384]{1,0:T(8,128)S(1)} %fusion.2, f32[384,384]{1,0:T(8,128)S(1)} %convert_select_fusion), kind=kOutput, calls=%fused_computation.51 | convolution fusion | flops 339738624 | bytes 1769472 | tf_op jit(solution)/shard_map/dot_general | solution.py:12
  37.2 0.0 collective-permute-done.3
  37.4 0.7 %fusion.23 = f32[384,384]{1,0:T(8,128)S(1)} fusion(f32[384,384]{1,0:T(8,128)S(1)} %convert_select_fusion.1, f32[384,384]{1,0:T(8,128)S(1)} %fusion.22), kind=kOutput, calls=%fused_computation.52 | convolution fusion | flops 339738624 | bytes 1769472 | tf_op jit(solution)/shard_map/dot_general | solution.py:8
  38.1 0.7 %convolution_bitcast_fusion = f32[384,384,1]{1,0,2:T(8,128)S(1)} fusion(f32[384,384]{1,0:T(8,128)S(1)} %fusion.23, f32[384,384]{1,0:T(8,128)S(1)} %convert_select_fusion.1), kind=kOutput, calls=%fused_computation | convolution fusion | flops 339738624 | bytes 1769472 | tf_op jit(solution)/shard_map/dot_general | solution.py:12
  38.9 0.0 collective-permute-done.10
  39.0 0.1 bitcast_select_fusion
  39.2 0.5 %fusion.9 = f32[4,48,384]{2,1,0:T(8,128)S(1)} fusion(f32[384,384,1]{1,0,2:T(8,128)S(1)} %convolution_bitcast_fusion, f32[4,48,384]{2,1,0:T(8,128)S(1)} %collective-permute-done.1, s32[4,1,48]{2,0,1:T(4,128)S(1)} %constant_dynamic-slice_fusion, pred[]{:T(512)S(6)} %ge.10), kind=kOutput, calls=%fused_computation.20 | convolution fusion | flops 170090496 | bytes 1180417 | tf_op jit(solution)/shard_map/dot_general | solution.py:8
  39.7 0.5 fusion
  40.2 2.1 %collective-permute-start.11 = (f32[48,384]{1,0:T(8,128)S(1)}, f32[48,384]{1,0:T(8,128)S(1)}, u32[]{:S(2)}, u32[]{:S(2)}) collective-permute-start(f32[48,384]{1,0:T(8,128)S(1)} %get-tuple-element.11), channel_id=1, source_target_pairs={{0,8},{4,12},{8,16},{12,20},{16,24},{20,28},{24,0},{28,4},{1,9},{5... | collective-permute-start | bytes 221192 | tf_op jit(solution)/shard_map/ppermute | solution.py:75
  42.3 2.5 %collective-permute-start.12 = (f32[48,384]{1,0:T(8,128)S(1)}, f32[48,384]{1,0:T(8,128)S(1)}, u32[]{:S(2)}, u32[]{:S(2)}) collective-permute-start(f32[48,384]{1,0:T(8,128)S(1)} %get-tuple-element.13), channel_id=1, source_target_pairs={{0,16},{4,20},{8,24},{12,28},{16,0},{20,4},{24,8},{28,12},{1,17},{... | collective-permute-start | bytes 221192 | tf_op jit(solution)/shard_map/ppermute | solution.py:75
  44.8 0.9 %collective-permute-start.13 = (f32[48,384]{1,0:T(8,128)S(1)}, f32[48,384]{1,0:T(8,128)S(1)}, u32[]{:S(2)}, u32[]{:S(2)}) collective-permute-start(f32[48,384]{1,0:T(8,128)S(1)} %get-tuple-element.12), channel_id=1, source_target_pairs={{0,24},{4,28},{8,0},{12,4},{16,8},{20,12},{24,16},{28,20},{1,25},{... | collective-permute-start | bytes 221192 | tf_op jit(solution)/shard_map/ppermute | solution.py:75
  45.6 1.1 %collective-permute-done.11 = f32[48,384]{1,0:T(8,128)S(1)} collective-permute-done((f32[48,384]{1,0:T(8,128)S(1)}, f32[48,384]{1,0:T(8,128)S(1)}, u32[]{:S(2)}, u32[]{:S(2)}) %collective-permute-start.11) | collective-permute-done | bytes 73760 | tf_op jit(solution)/shard_map/ppermute | solution.py:75
  46.7 1.5 %collective-permute-done.12 = f32[48,384]{1,0:T(8,128)S(1)} collective-permute-done((f32[48,384]{1,0:T(8,128)S(1)}, f32[48,384]{1,0:T(8,128)S(1)}, u32[]{:S(2)}, u32[]{:S(2)}) %collective-permute-start.12) | collective-permute-done | bytes 73760 | tf_op jit(solution)/shard_map/ppermute | solution.py:75
  48.2 0.9 %collective-permute-done.13 = f32[48,384]{1,0:T(8,128)S(1)} collective-permute-done((f32[48,384]{1,0:T(8,128)S(1)}, f32[48,384]{1,0:T(8,128)S(1)}, u32[]{:S(2)}, u32[]{:S(2)}) %collective-permute-start.13) | collective-permute-done | bytes 73760 | tf_op jit(solution)/shard_map/ppermute | solution.py:75
  49.1 0.7 %fusion.18 = f32[48,384]{1,0:T(8,128)} fusion(f32[48,384]{1,0:T(8,128)S(1)} %collective-permute-done.13, f32[48,384]{1,0:T(8,128)S(1)} %collective-permute-done.12, f32[48,384]{1,0:T(8,128)S(1)} %collective-permute-done.11, f32[4,48,384]{2,1,0:T(8,128)S(1)} %fusion, s32[]{:T(128)S(6)} %select_n.169), kind=kLoop, calls=%fused_computation.38 | loop fusion | flops 55296 | bytes 368644 | tf_op jit(solution)/shard_map/add | solution.py:75
  (20 shorter events, 0.6 us)
Async XLA Ops:
  0.0 16.3 %collective-permute-start = (f32[384,384]{1,0:T(8,128)}, f32[384,384]{1,0:T(8,128)S(1)}, u32[]{:S(2)}, u32[]{:S(2)}) collective-permute-start(f32[384,384]{1,0:T(8,128)} %bitcast.70), channel_id=1, source_target_pairs={{0,4},{4,0},{8,12},{12,8},{16,20},{20,16},{24,28},{28,24},{1,5},{5... | collective-permute-start | bytes 1769480 | tf_op jit(solution)/shard_map/ppermute | solution.py:32
  0.5 9.6 %collective-permute-start.6 = (f32[96,384]{1,0:T(8,128)}, f32[96,384]{1,0:T(8,128)S(1)}, u32[]{:S(2)}, u32[]{:S(2)}) collective-permute-start(f32[96,384]{1,0:T(8,128)} %bitcast.72), channel_id=1, source_target_pairs={{0,1},{1,2},{2,3},{3,0},{4,5},{5,6},{6,7},{7,4},{8,9},{9,10},{10,1... | collective-permute-start | bytes 442376 | tf_op jit(solution)/shard_map/ppermute | solution.py:40
  3.1 13.1 %collective-permute-start.7 = (f32[96,384]{1,0:T(8,128)}, f32[96,384]{1,0:T(8,128)S(1)}, u32[]{:S(2)}, u32[]{:S(2)}) collective-permute-start(f32[96,384]{1,0:T(8,128)} %bitcast.73), channel_id=1, source_target_pairs={{0,2},{1,3},{2,0},{3,1},{4,6},{5,7},{6,4},{7,5},{8,10},{9,11},{10,... | collective-permute-start | bytes 442376 | tf_op jit(solution)/shard_map/ppermute | solution.py:40
  5.6 10.6 %collective-permute-start.8 = (f32[96,384]{1,0:T(8,128)}, f32[96,384]{1,0:T(8,128)S(1)}, u32[]{:S(2)}, u32[]{:S(2)}) collective-permute-start(f32[96,384]{1,0:T(8,128)} %bitcast.74), channel_id=1, source_target_pairs={{0,3},{1,0},{2,1},{3,2},{4,7},{5,4},{6,5},{7,6},{8,11},{9,8},{10,9... | collective-permute-start | bytes 442376 | tf_op jit(solution)/shard_map/ppermute | solution.py:40
  7.0 0.9 %copy-start.1 = (f32[1,96,384]{2,1,0:T(8,128)S(1)}, f32[1,96,384]{2,1,0:T(8,128)}, u32[]{:S(2)}) copy-start(f32[1,96,384]{2,1,0:T(8,128)} %param.3) | copy-start | bytes 442372
  7.9 8.4 %copy-start = (f32[1,384,384]{2,1,0:T(8,128)S(1)}, f32[1,384,384]{2,1,0:T(8,128)}, u32[]{:S(2)}) copy-start(f32[1,384,384]{2,1,0:T(8,128)} %param.2) | copy-start | bytes 1769476
  16.2 12.0 %collective-permute-start.9 = (f32[384,384]{1,0:T(8,128)S(1)}, f32[384,384]{1,0:T(8,128)S(1)}, u32[]{:S(2)}, u32[]{:S(2)}) collective-permute-start(f32[384,384]{1,0:T(8,128)S(1)} %constant_dynamic-update-slice_fusion), channel_id=1, source_target_pairs={{0,4},{4,0},{8,12},{12,8},{16,20},{20,16},{24,28},{28,24},{1,5},{5... | collective-permute-start | bytes 1769480 | tf_op jit(solution)/shard_map/ppermute | solution.py:54
  17.5 10.8 %collective-permute-start.4 = (f32[4,48,384]{2,1,0:T(8,128)S(1)}, f32[4,48,384]{2,1,0:T(8,128)S(1)}, u32[]{:S(2)}, u32[]{:S(2)}) collective-permute-start(f32[4,48,384]{2,1,0:T(8,128)S(1)} %dynamic-slice_bitcast_fusion), channel_id=1, source_target_pairs={{0,8},{4,12},{8,16},{12,20},{16,24},{20,28},{1,9},{5,13},{9,17},{1... | collective-permute-start | bytes 884744 | tf_op jit(solution)/shard_map/ppermute | solution.py:52
  21.1 14.0 %collective-permute-start.2 = (f32[4,48,384]{2,1,0:T(8,128)S(1)}, f32[4,48,384]{2,1,0:T(8,128)S(1)}, u32[]{:S(2)}, u32[]{:S(2)}) collective-permute-start(f32[4,48,384]{2,1,0:T(8,128)S(1)} %dynamic-slice_bitcast_fusion), channel_id=1, source_target_pairs={{0,16},{4,20},{8,24},{12,28},{1,17},{5,21},{9,25},{13,29},{2,18},{... | collective-permute-start | bytes 884744 | tf_op jit(solution)/shard_map/ppermute | solution.py:52
  24.5 10.6 %collective-permute-start.1 = (f32[4,48,384]{2,1,0:T(8,128)S(1)}, f32[4,48,384]{2,1,0:T(8,128)S(1)}, u32[]{:S(2)}, u32[]{:S(2)}) collective-permute-start(f32[4,48,384]{2,1,0:T(8,128)S(1)} %dynamic-slice_bitcast_fusion), channel_id=1, source_target_pairs={{0,24},{4,28},{1,25},{5,29},{2,26},{6,30},{3,27},{7,31}} | collective-permute-start | bytes 884744 | tf_op jit(solution)/shard_map/ppermute | solution.py:52
  28.3 7.3 %collective-permute-start.5 = (f32[4,48,384]{2,1,0:T(8,128)S(1)}, f32[4,48,384]{2,1,0:T(8,128)S(1)}, u32[]{:S(2)}, u32[]{:S(2)}) collective-permute-start(f32[4,48,384]{2,1,0:T(8,128)S(1)} %collective-permute-done.4), channel_id=1, source_target_pairs={{0,4},{4,0},{8,12},{12,8},{16,20},{20,16},{24,28},{28,24},{1,5},{5... | collective-permute-start | bytes 884744 | tf_op jit(solution)/shard_map/ppermute | solution.py:62
  35.1 2.2 %collective-permute-start.3 = (f32[4,48,384]{2,1,0:T(8,128)S(1)}, f32[4,48,384]{2,1,0:T(8,128)S(1)}, u32[]{:S(2)}, u32[]{:S(2)}) collective-permute-start(f32[4,48,384]{2,1,0:T(8,128)S(1)} %collective-permute-done.2), channel_id=1, source_target_pairs={{0,4},{4,0},{8,12},{12,8},{16,20},{20,16},{24,28},{28,24},{1,5},{5... | collective-permute-start | bytes 884744 | tf_op jit(solution)/shard_map/ppermute | solution.py:62
  35.1 3.8 %collective-permute-start.10 = (f32[4,48,384]{2,1,0:T(8,128)S(1)}, f32[4,48,384]{2,1,0:T(8,128)S(1)}, u32[]{:S(2)}, u32[]{:S(2)}) collective-permute-start(f32[4,48,384]{2,1,0:T(8,128)S(1)} %collective-permute-done.1), channel_id=1, source_target_pairs={{0,4},{4,0},{8,12},{12,8},{16,20},{20,16},{24,28},{28,24},{1,5},{5... | collective-permute-start | bytes 884744 | tf_op jit(solution)/shard_map/ppermute | solution.py:62
  40.2 6.6 %collective-permute-start.11 = (f32[48,384]{1,0:T(8,128)S(1)}, f32[48,384]{1,0:T(8,128)S(1)}, u32[]{:S(2)}, u32[]{:S(2)}) collective-permute-start(f32[48,384]{1,0:T(8,128)S(1)} %get-tuple-element.11), channel_id=1, source_target_pairs={{0,8},{4,12},{8,16},{12,20},{16,24},{20,28},{24,0},{28,4},{1,9},{5... | collective-permute-start | bytes 221192 | tf_op jit(solution)/shard_map/ppermute | solution.py:75
  42.3 5.9 %collective-permute-start.12 = (f32[48,384]{1,0:T(8,128)S(1)}, f32[48,384]{1,0:T(8,128)S(1)}, u32[]{:S(2)}, u32[]{:S(2)}) collective-permute-start(f32[48,384]{1,0:T(8,128)S(1)} %get-tuple-element.13), channel_id=1, source_target_pairs={{0,16},{4,20},{8,24},{12,28},{16,0},{20,4},{24,8},{28,12},{1,17},{... | collective-permute-start | bytes 221192 | tf_op jit(solution)/shard_map/ppermute | solution.py:75
  44.8 4.4 %collective-permute-start.13 = (f32[48,384]{1,0:T(8,128)S(1)}, f32[48,384]{1,0:T(8,128)S(1)}, u32[]{:S(2)}, u32[]{:S(2)}) collective-permute-start(f32[48,384]{1,0:T(8,128)S(1)} %get-tuple-element.12), channel_id=1, source_target_pairs={{0,24},{4,28},{8,0},{12,4},{16,8},{20,12},{24,16},{28,20},{1,25},{... | collective-permute-start | bytes 221192 | tf_op jit(solution)/shard_map/ppermute | solution.py:75

commit v2 on v1

v2 whole, which is shorter than its diff:
```python
import functools

import jax
import jax.numpy as jnp
from jax import lax
from jax.experimental import pallas as pl
from jax.experimental.pallas import tpu as pltpu
from jax.sharding import PartitionSpec as P

VMEM = pl.BlockSpec(memory_space=pltpu.VMEM)
F32, BF16 = jnp.float32, jnp.bfloat16


def product(left, right, left_dim, right_dim):
    dims = (((left_dim,), (right_dim,)), ((), ()))
    return lax.dot_general(left, right, dims, precision=lax.Precision.HIGH, preferred_element_type=F32)


def parts(x):
    high = x.astype(BF16)
    return high, (x - high.astype(F32)).astype(BF16)


def mul(left, right, right_dim=0):
    dims = (((1,), (right_dim,)), ((), ()))
    dot = functools.partial(lax.dot_general, dimension_numbers=dims, preferred_element_type=F32)
    return dot(left[0], right[0]) + (dot(left[0], right[1]) + dot(left[1], right[0]))


def call(kernel, outs, operands, scratch=(), flops=0):
    outs = tuple(jax.ShapeDtypeStruct(shape, F32) for shape in outs)
    return pl.pallas_call(
        kernel,
        out_shape=outs,
        in_specs=[VMEM] * len(operands),
        out_specs=(VMEM,) * len(outs),
        scratch_shapes=[pltpu.VMEM(shape, F32) for shape in scratch],
        cost_estimate=pl.CostEstimate(flops=flops, bytes_accessed=0, transcendentals=0),
        compiler_params=pltpu.CompilerParams(vmem_limit_bytes=12 * 2**20),
    )(*operands)


def pair_kernel(own, other, half, even_t, work):
    core = lax.rem(lax.axis_index("tm"), 2)
    chips, rows, order_dim = half.shape

    def run(even, odd):
        even_t[...] = even[...].T
        for k in range(chips):
            start = pl.multiple_of((2 * k + core) * rows, 8)
            work[k] = even_t[pl.ds(start, rows), :]
        left = parts(work[...].reshape(chips * rows, order_dim))
        half[...] = mul(left, parts(odd[...]), 1).reshape(half.shape)

    pl.when(core == 0)(lambda: run(own, other))
    pl.when(core == 1)(lambda: run(other, own))


def fill(whole, core, mine, theirs):
    whole[:, core] = mine[...]
    whole[:, 1 - core] = theirs[...]


def chain_kernel(chips, *refs):
    count = chips - 2
    mine, theirs, (out, whole) = refs[:count], refs[count : 2 * count], refs[2 * count :]
    place = lax.axis_index("tm")
    chip, core = place // 2, lax.rem(place, 2)
    order_dim = out.shape[0]
    for shift in range(1, chips - 1):

        @pl.when(chip > shift)
        def _(shift=shift):
            fill(whole, core, mine[shift - 1], theirs[shift - 1])
            step = whole[...].reshape(order_dim, order_dim)
            if shift == 1:
                out[...] = step
            else:
                out[...] = mul(parts(step), parts(out[...]))


def local_kernel(planes, *refs):
    mine, theirs = refs[:planes], refs[planes : 2 * planes]
    even_t, chain, out, both = refs[2 * planes :]
    place, plane = lax.axis_index("tm"), lax.axis_index("group")
    chip, core = place // 2, lax.rem(place, 2)
    rows = mine[0].shape[0]
    for shift in range(planes):
        start = pl.multiple_of(lax.rem(plane + planes - shift, planes) * rows, 8)
        both[core, pl.ds(start, rows), :] = mine[shift][...]
        both[1 - core, pl.ds(start, rows), :] = theirs[shift][...]
    left = parts(even_t[...])
    total = both[0] + mul(parts(mul(left, parts(both[1]))), left, 1)

    @pl.when(chip < 2)
    def _():
        out[...] = total

    @pl.when(chip >= 2)
    def _():
        left = parts(chain[...])
        out[...] = mul(parts(mul(left, parts(total))), left, 1)


def last_kernel(mine, theirs, total, out, whole):
    place = lax.axis_index("tm")
    chip, core = place // 2, lax.rem(place, 2)
    order_dim = total.shape[0]
    chips, rows = out.shape[:2]

    @pl.when(chip == 0)
    def _():
        for k in range(chips):
            out[k] = total[pl.ds(pl.multiple_of((2 * k + core) * rows, 8), rows), :]

    @pl.when(chip > 0)
    def _():
        fill(whole, core, mine, theirs)
        right = parts(whole[...].reshape(order_dim, order_dim))
        left = parts(mine[...].reshape(order_dim // 2, order_dim))
        out[...] = mul(parts(mul(left, parts(total[...]))), right, 1).reshape(out.shape)


def body(propagators, perturbation):
    devices = lax.axis_size("tm")
    planes = lax.axis_size("group")
    chips = devices // 2
    order_dim = propagators.shape[1]
    out_rows = order_dim // devices
    place = lax.axis_index("tm")
    chip = place // 2
    partner = [(i, i ^ 1) for i in range(devices)]
    swap = lambda x: lax.ppermute(x, "tm", partner)
    cube = 2 * order_dim**3

    def chip_pairs(pairs):
        return [(2 * i + c, 2 * j + c) for i, j in pairs for c in range(2)]

    own = propagators[0]
    rows = perturbation[0]
    other = swap(own)
    blocks = [rows]
    for shift in range(1, planes):
        blocks.append(lax.ppermute(rows, "group", [(i, (i + shift) % planes) for i in range(planes)]))
    half_shape = (chips, out_rows, order_dim)
    half, even_t = call(pair_kernel, [half_shape, own.shape], [own, other], [half_shape], 2 * cube)

    sent = []
    for shift in range(1, chips - 1):
        sent.append(lax.ppermute(half, "tm", chip_pairs([(i, i + shift) for i in range(1, chips - shift)])))
    first = []
    for shift in range(1, chips):
        first.append(lax.ppermute(half, "tm", chip_pairs([(0, shift)])))
    sent_other = []
    for shift in range(1, chips - 1):
        sent_other.append(swap(sent[shift - 1]))
    (chain,) = call(
        functools.partial(chain_kernel, chips), [own.shape], sent + sent_other,
        [(chips, 2, out_rows, order_dim)], 3 * cube,
    )
    blocks_other = []
    for shift in range(planes):
        blocks_other.append(swap(blocks[shift]))
    (total,) = call(
        functools.partial(local_kernel, planes), [own.shape],
        blocks + blocks_other + [even_t, chain], [(2,) + own.shape], 12 * cube,
    )
    mine = first[0]
    for shift in range(2, chips):
        mine = jnp.where(chip == shift, first[shift - 1], mine)
    theirs = swap(mine)
    (terms,) = call(last_kernel, [half_shape], [mine, theirs, total], [(chips, 2, out_rows, order_dim)], 3 * cube)
    out = lax.dynamic_index_in_dim(terms, chip, 0, False)
    for shift in range(chips - 1, 0, -1):
        block = lax.dynamic_index_in_dim(terms, chip ^ shift, 0, False)
        out = out + lax.ppermute(block, "tm", [(i, i ^ (2 * shift)) for i in range(devices)])
    return out


def plain_body(propagators, perturbation):
    devices = lax.axis_size("tm")
    planes = lax.axis_size("group")
    chips = devices // 2
    order_dim = propagators.shape[1]
    block_rows = perturbation.shape[1]
    out_rows = order_dim // devices
    place = lax.axis_index("tm")
    plane = lax.axis_index("group")
    chip, core = place // 2, place % 2
    partner = [(i, i ^ 1) for i in range(devices)]
    identity = jnp.eye(order_dim, dtype=F32)

    def half_of(whole):
        split = whole.reshape(chips, 2, out_rows, order_dim)
        return lax.dynamic_index_in_dim(split, core, 1, False)

    def by_core(mine, theirs):
        return jnp.where(core == 0, mine, theirs), jnp.where(core == 0, theirs, mine)

    own = propagators[0]
    even, odd = by_core(own, lax.ppermute(own, "tm", partner))
    rows = perturbation[0]
    full = jnp.zeros((order_dim, order_dim), F32)
    for shift in range(planes):
        got = rows
        if shift:
            got = lax.ppermute(rows, "group", [(i, (i + shift) % planes) for i in range(planes)])
        full = lax.dynamic_update_slice_in_dim(full, got, (plane - shift) % planes * block_rows, 0)
    half = half_of(product(even, odd, 0, 1))
    full_even, full_odd = by_core(full, lax.ppermute(full, "tm", partner))
    total = full_even + product(even, product(full_odd, even, 1, 0), 0, 0)
    for shift in range(1, chips):
        got = lax.ppermute(half, "tm", [(i, i + 2 * shift) for i in range(devices - 2 * shift)])
        mine = jnp.where(chip >= shift, got, half_of(identity))
        theirs = lax.ppermute(mine, "tm", partner)
        whole = jnp.stack(by_core(mine, theirs), 1).reshape(order_dim, order_dim)
        total = product(product(whole, total, 1, 0), whole, 1, 1)
    terms = half_of(total)
    out = lax.dynamic_index_in_dim(terms, chip, 0, False)
    for shift in range(1, chips):
        block = lax.dynamic_index_in_dim(terms, (chip + shift) % chips, 0, False)
        out = out + lax.ppermute(block, "tm", [(i, (i + 2 * shift) % devices) for i in range(devices)])
    return out


def solution(mesh):
    in_specs = (P("tm", None, None), P("tm", "group", None))
    out_specs = P("tm", None)
    chips, planes = mesh.shape["tm"] // 2, mesh.shape["group"]

    def step(propagators, perturbation):
        order_dim = propagators.shape[1]
        tiled = order_dim // planes % 8 == 0 and order_dim // (2 * chips) % 8 == 0
        power = chips & (chips - 1) == 0 and chips > 2
        plan = body if tiled and power else plain_body
        return jax.shard_map(plan, mesh=mesh, in_specs=in_specs, out_specs=out_specs, check_vma=False)(
            propagators, perturbation
        )

    return step
```

time: 50.5 us -> 53.8 us (1.065)
  the two profiles are of different devices: /device:TPU:0 before, /device:TPU:20 now
where the time goes in v2:
time: 53.8 us; the launch traced here: 53.5 us
  waiting for transfers between devices  26.7 us (50%)
  starting transfers between devices  19.9 us (37%)
  Pallas kernels  5.08 us (9%)
  local copies, waits for them, and re-layouts  1.09 us (2%)
  other arithmetic  0.69 us (1%)
    ppermute x3, starting transfers between devices, body(): lax.ppermute(block, 'tm', [(i, i ^ 2 * shift) for i in range(devices)])  9.6 us
    ppermute x3, waiting for transfers between devices, body(): lax.ppermute(rows, 'group', [(i, (i + shift) % planes) for i in range(pla...  8.34 us
    ppermute x3, waiting for transfers between devices, body(): first.append(lax.ppermute(half, 'tm', chip_pairs([(0, shift)])))  5.37 us
    ppermute x2, waiting for transfers between devices, body(): lax.ppermute(half, 'tm', chip_pairs([(i, i + shift) for i in range(1, chi...  5.18 us
    pallas_call x4, Pallas kernels, call(): pl.pallas_call(kernel, out_shape=outs, in_specs=[VMEM] * len(operands), o...  5.08 us
    ppermute x3, waiting for transfers between devices, body(): lax.ppermute(block, 'tm', [(i, i ^ 2 * shift) for i in range(devices)])  4.35 us
    ppermute x2, starting transfers between devices, body(): lax.ppermute(half, 'tm', chip_pairs([(i, i + shift) for i in range(1, chi...  4.07 us
    ppermute x8, waiting for transfers between devices, body(): swap = lambda x: lax.ppermute(x, 'tm', partner)  3.42 us
  transfers between devices with their start and end apart: 19, of which 10 were waited for; matrix products, arithmetic and copies ran while one was open for 0% of the time, Pallas kernels for 6%

profile of v2, /device:TPU:20, one launch (start us, length us, event | category | flops | bytes accessed | tf_op | source)
XLA Modules:
  0.0 53.5 jit_solution(5303709913021893312)
XLA Ops:
  0.0 0.0 collective-permute-start
  0.0 2.2 %collective-permute-done.other = f32[384,384]{1,0:T(8,128)S(1)} collective-permute-done((f32[384,384]{1,0:T(8,128)}, f32[384,384]{1,0:T(8,128)S(1)}, u32[]{:S(2)}, u32[]{:S(2)}) %collective-permute-start) | collective-permute-done | bytes 589856 | tf_op jit(solution)/shard_map/ppermute | solution.py:133
  2.2 0.0 copy-start
  2.2 1.1 %copy-done = f32[1,384,384]{2,1,0:T(8,128)S(1)} copy-done((f32[1,384,384]{2,1,0:T(8,128)S(1)}, f32[1,384,384]{2,1,0:T(8,128)}, u32[]{:S(2)}) %copy-start) | copy-done | bytes 589848
  3.3 0.0 copy-start.1
  3.3 0.7 %shard_map.28 = (f32[4,48,384]{2,1,0:T(8,128)S(1)}, f32[384,384]{1,0:T(8,128)S(1)}) custom-call(f32[384,384]{1,0:T(8,128)S(1)} %bitcast.15, f32[384,384]{1,0:T(8,128)S(1)} %collective-permute-done.other), custom_call_target="tpu_custom_call" | custom-call | flops 226492416 | tf_op jit(solution)/shard_map/pallas_call | solution.py:32
  4.0 3.4 %collective-permute-start.12 = (f32[4,48,384]{2,1,0:T(8,128)S(1)}, f32[4,48,384]{2,1,0:T(8,128)S(1)}, u32[]{:S(2)}, u32[]{:S(2)}) collective-permute-start(f32[4,48,384]{2,1,0:T(8,128)S(1)} %get-tuple-element.7), channel_id=1, source_target_pairs={{8,16},{12,20},{16,24},{20,28},{9,17},{13,21},{17,25},{21,29},{10,... | collective-permute-start | bytes 884744 | tf_op jit(solution)/shard_map/ppermute | solution.py:150
  7.4 0.7 %collective-permute-start.13 = (f32[4,48,384]{2,1,0:T(8,128)S(1)}, f32[4,48,384]{2,1,0:T(8,128)S(1)}, u32[]{:S(2)}, u32[]{:S(2)}) collective-permute-start(f32[4,48,384]{2,1,0:T(8,128)S(1)} %get-tuple-element.7), channel_id=1, source_target_pairs={{8,24},{12,28},{9,25},{13,29},{10,26},{14,30},{11,27},{15,31}} | collective-permute-start | bytes 884744 | tf_op jit(solution)/shard_map/ppermute | solution.py:150
  8.1 0.7 %collective-permute-start.1 = (f32[4,48,384]{2,1,0:T(8,128)S(1)}, f32[4,48,384]{2,1,0:T(8,128)S(1)}, u32[]{:S(2)}, u32[]{:S(2)}) collective-permute-start(f32[4,48,384]{2,1,0:T(8,128)S(1)} %get-tuple-element.7), channel_id=1, source_target_pairs={{0,24},{4,28},{1,25},{5,29},{2,26},{6,30},{3,27},{7,31}} | collective-permute-start | bytes 884744 | tf_op jit(solution)/shard_map/ppermute | solution.py:153
  8.8 1.3 %collective-permute-start.2 = (f32[4,48,384]{2,1,0:T(8,128)S(1)}, f32[4,48,384]{2,1,0:T(8,128)S(1)}, u32[]{:S(2)}, u32[]{:S(2)}) collective-permute-start(f32[4,48,384]{2,1,0:T(8,128)S(1)} %get-tuple-element.7), channel_id=1, source_target_pairs={{0,16},{4,20},{1,17},{5,21},{2,18},{6,22},{3,19},{7,23}} | collective-permute-start | bytes 884744 | tf_op jit(solution)/shard_map/ppermute | solution.py:153
  10.1 0.7 %collective-permute-start.3 = (f32[4,48,384]{2,1,0:T(8,128)S(1)}, f32[4,48,384]{2,1,0:T(8,128)S(1)}, u32[]{:S(2)}, u32[]{:S(2)}) collective-permute-start(f32[4,48,384]{2,1,0:T(8,128)S(1)} %get-tuple-element.7), channel_id=1, source_target_pairs={{0,8},{4,12},{1,9},{5,13},{2,10},{6,14},{3,11},{7,15}} | collective-permute-start | bytes 884744 | tf_op jit(solution)/shard_map/ppermute | solution.py:153
  10.8 5.2 %collective-permute-done.12.refs_0_ = f32[4,48,384]{2,1,0:T(8,128)S(1)} collective-permute-done((f32[4,48,384]{2,1,0:T(8,128)S(1)}, f32[4,48,384]{2,1,0:T(8,128)S(1)}, u32[]{:S(2)}, u32[]{:S(2)}) %collective-permute-start.12) | collective-permute-done | bytes 294944 | tf_op jit(solution)/shard_map/ppermute | solution.py:150
  15.9 0.0 collective-permute-start.14
  15.9 0.0 collective-permute-done.13.refs_1_
  16.0 0.5 collective-permute-start.15
  16.5 0.0 collective-permute-done.1
  16.5 0.0 copy-done.1
  16.5 0.3 collective-permute-start.6
  16.8 5.4 %collective-permute-done.2 = f32[4,48,384]{2,1,0:T(8,128)S(1)} collective-permute-done((f32[4,48,384]{2,1,0:T(8,128)S(1)}, f32[4,48,384]{2,1,0:T(8,128)S(1)}, u32[]{:S(2)}, u32[]{:S(2)}) %collective-permute-start.2) | collective-permute-done | bytes 294944 | tf_op jit(solution)/shard_map/ppermute | solution.py:153
  22.2 0.5 collective-permute-start.7
  22.6 0.0 collective-permute-done.3
  22.6 1.6 %collective-permute-start.5 = (f32[96,384]{1,0:T(8,128)S(1)}, f32[96,384]{1,0:T(8,128)S(1)}, u32[]{:S(2)}, u32[]{:S(2)}) collective-permute-start(f32[96,384]{1,0:T(8,128)S(1)} %bitcast.18), channel_id=1, source_target_pairs={{0,1},{1,2},{2,3},{3,0},{4,5},{5,6},{6,7},{7,4},{8,9},{9,10},{10,1... | collective-permute-start | bytes 442376 | tf_op jit(solution)/shard_map/ppermute | solution.py:144
  24.2 0.0 collective-permute-done.6.refs_2_
  24.3 0.1 collective-permute-start.4
  24.3 3.7 %collective-permute-done.7.refs_3_ = f32[96,384]{1,0:T(8,128)S(1)} collective-permute-done((f32[96,384]{1,0:T(8,128)S(1)}, f32[96,384]{1,0:T(8,128)S(1)}, u32[]{:S(2)}, u32[]{:S(2)}) %collective-permute-start.7) | collective-permute-done | bytes 147488 | tf_op jit(solution)/shard_map/ppermute | solution.py:144
  28.0 0.0 collective-permute-start.8
  28.0 4.6 %collective-permute-done.5.refs_1_ = f32[96,384]{1,0:T(8,128)S(1)} collective-permute-done((f32[96,384]{1,0:T(8,128)S(1)}, f32[96,384]{1,0:T(8,128)S(1)}, u32[]{:S(2)}, u32[]{:S(2)}) %collective-permute-start.5) | collective-permute-done | bytes 147488 | tf_op jit(solution)/shard_map/ppermute | solution.py:144
  32.7 0.0 collective-permute-start.10
  32.7 0.0 collective-permute-done.14.refs_2_
  32.7 0.5 collective-permute-start.11
  33.2 0.0 collective-permute-done.15.refs_3_
  33.2 0.1 collective-permute-start.9
  33.3 0.1 shard_map.29.refs_9_
  33.4 0.0 collective-permute-done.8.refs_4_
  33.4 0.7 %collective-permute-done.10.refs_6_ = f32[96,384]{1,0:T(8,128)S(1)} collective-permute-done((f32[96,384]{1,0:T(8,128)S(1)}, f32[96,384]{1,0:T(8,128)S(1)}, u32[]{:S(2)}, u32[]{:S(2)}) %collective-permute-start.10) | collective-permute-done | bytes 147488 | tf_op jit(solution)/shard_map/ppermute | solution.py:133
  34.0 0.2 collective-permute-done.11.refs_7_
  34.3 0.3 collective-permute-done.9.refs_5_
  34.6 3.3 %shard_map.30.total = f32[384,384]{1,0:T(8,128)S(1)} custom-call(f32[96,384]{1,0:T(8,128)S(1)} %bitcast.20, f32[96,384]{1,0:T(8,128)S(1)} %collective-permute-done.5.refs_1_, f32[96,384]{1,0:T(8,128)S(1)} %collective-permute-done.6.refs_2_, f32[96,384]{1,0:T(8,128)S(1)} %collective-permute-done.7.refs_3_, f32[96,384]{1,0:T(8,128)S(1)} %collective-permute-done.8.refs_4_, ...), custom_call_target="tpu_custom_call" | custom-call | flops 1358954496 | tf_op jit(solution)/shard_map/pallas_call | solution.py:32
  37.8 0.0 collective-permute-done.4.theirs
  37.9 1.0 %shard_map.31 = f32[4,48,384]{2,1,0:T(8,128)S(1)} custom-call(f32[4,48,384]{2,1,0:T(8,128)S(1)} %select_select_fusion.mine, f32[4,48,384]{2,1,0:T(8,128)S(1)} %collective-permute-done.4.theirs, f32[384,384]{1,0:T(8,128)S(1)} %shard_map.30.total), custom_call_target="tpu_custom_call" | custom-call | flops 339738624 | tf_op jit(solution)/shard_map/pallas_call | solution.py:32
  38.9 5.6 %collective-permute-start.16 = (f32[48,384]{1,0:T(8,128)S(1)}, f32[48,384]{1,0:T(8,128)S(1)}, u32[]{:S(2)}, u32[]{:S(2)}) collective-permute-start(f32[48,384]{1,0:T(8,128)S(1)} %get-tuple-element.9), channel_id=1, source_target_pairs={{0,24},{4,28},{8,16},{12,20},{16,8},{20,12},{24,0},{28,4},{1,25},{... | collective-permute-start | bytes 221192 | tf_op jit(solution)/shard_map/ppermute | solution.py:176
  44.5 4.0 %collective-permute-start.17 = (f32[48,384]{1,0:T(8,128)S(1)}, f32[48,384]{1,0:T(8,128)S(1)}, u32[]{:S(2)}, u32[]{:S(2)}) collective-permute-start(f32[48,384]{1,0:T(8,128)S(1)} %get-tuple-element.11), channel_id=1, source_target_pairs={{0,16},{4,20},{8,24},{12,28},{16,0},{20,4},{24,8},{28,12},{1,17},{... | collective-permute-start | bytes 221192 | tf_op jit(solution)/shard_map/ppermute | solution.py:176
  48.5 0.0 collective-permute-start.18
  48.5 0.0 collective-permute-done.16
  48.5 2.4 %collective-permute-done.17 = f32[48,384]{1,0:T(8,128)S(1)} collective-permute-done((f32[48,384]{1,0:T(8,128)S(1)}, f32[48,384]{1,0:T(8,128)S(1)}, u32[]{:S(2)}, u32[]{:S(2)}) %collective-permute-start.17) | collective-permute-done | bytes 73760 | tf_op jit(solution)/shard_map/ppermute | solution.py:176
  50.9 2.0 %collective-permute-done.18 = f32[48,384]{1,0:T(8,128)S(1)} collective-permute-done((f32[48,384]{1,0:T(8,128)S(1)}, f32[48,384]{1,0:T(8,128)S(1)}, u32[]{:S(2)}, u32[]{:S(2)}) %collective-permute-start.18) | collective-permute-done | bytes 73760 | tf_op jit(solution)/shard_map/ppermute | solution.py:176
  52.9 0.7 %fusion.1 = f32[48,384]{1,0:T(8,128)} fusion(f32[48,384]{1,0:T(8,128)S(1)} %collective-permute-done.18, f32[48,384]{1,0:T(8,128)S(1)} %collective-permute-done.17, f32[48,384]{1,0:T(8,128)S(1)} %collective-permute-done.16, f32[4,48,384]{2,1,0:T(8,128)S(1)} %shard_map.31, s32[]{:T(128)S(6)} %select_n.37), kind=kLoop, calls=%fused_computation.3 | loop fusion | flops 55296 | bytes 368644 | tf_op jit(solution)/shard_map/add | solution.py:176
  (2 shorter events, 0.1 us)
Async XLA Ops:
  0.0 2.2 %collective-permute-start = (f32[384,384]{1,0:T(8,128)}, f32[384,384]{1,0:T(8,128)S(1)}, u32[]{:S(2)}, u32[]{:S(2)}) collective-permute-start(f32[384,384]{1,0:T(8,128)} %bitcast.14), channel_id=1, source_target_pairs={{0,4},{4,0},{8,12},{12,8},{16,20},{20,16},{24,28},{28,24},{1,5},{5... | collective-permute-start | bytes 1769480 | tf_op jit(solution)/shard_map/ppermute | solution.py:133
  2.2 1.1 %copy-start = (f32[1,384,384]{2,1,0:T(8,128)S(1)}, f32[1,384,384]{2,1,0:T(8,128)}, u32[]{:S(2)}) copy-start(f32[1,384,384]{2,1,0:T(8,128)} %param.2) | copy-start | bytes 1769476
  3.3 13.2 %copy-start.1 = (f32[1,96,384]{2,1,0:T(8,128)S(1)}, f32[1,96,384]{2,1,0:T(8,128)}, u32[]{:S(2)}) copy-start(f32[1,96,384]{2,1,0:T(8,128)} %param.3) | copy-start | bytes 442372
  4.0 11.9 %collective-permute-start.12 = (f32[4,48,384]{2,1,0:T(8,128)S(1)}, f32[4,48,384]{2,1,0:T(8,128)S(1)}, u32[]{:S(2)}, u32[]{:S(2)}) collective-permute-start(f32[4,48,384]{2,1,0:T(8,128)S(1)} %get-tuple-element.7), channel_id=1, source_target_pairs={{8,16},{12,20},{16,24},{20,28},{9,17},{13,21},{17,25},{21,29},{10,... | collective-permute-start | bytes 884744 | tf_op jit(solution)/shard_map/ppermute | solution.py:150
  7.4 8.5 %collective-permute-start.13 = (f32[4,48,384]{2,1,0:T(8,128)S(1)}, f32[4,48,384]{2,1,0:T(8,128)S(1)}, u32[]{:S(2)}, u32[]{:S(2)}) collective-permute-start(f32[4,48,384]{2,1,0:T(8,128)S(1)} %get-tuple-element.7), channel_id=1, source_target_pairs={{8,24},{12,28},{9,25},{13,29},{10,26},{14,30},{11,27},{15,31}} | collective-permute-start | bytes 884744 | tf_op jit(solution)/shard_map/ppermute | solution.py:150
  8.1 8.4 %collective-permute-start.1 = (f32[4,48,384]{2,1,0:T(8,128)S(1)}, f32[4,48,384]{2,1,0:T(8,128)S(1)}, u32[]{:S(2)}, u32[]{:S(2)}) collective-permute-start(f32[4,48,384]{2,1,0:T(8,128)S(1)} %get-tuple-element.7), channel_id=1, source_target_pairs={{0,24},{4,28},{1,25},{5,29},{2,26},{6,30},{3,27},{7,31}} | collective-permute-start | bytes 884744 | tf_op jit(solution)/shard_map/ppermute | solution.py:153
  8.8 13.4 %collective-permute-start.2 = (f32[4,48,384]{2,1,0:T(8,128)S(1)}, f32[4,48,384]{2,1,0:T(8,128)S(1)}, u32[]{:S(2)}, u32[]{:S(2)}) collective-permute-start(f32[4,48,384]{2,1,0:T(8,128)S(1)} %get-tuple-element.7), channel_id=1, source_target_pairs={{0,16},{4,20},{1,17},{5,21},{2,18},{6,22},{3,19},{7,23}} | collective-permute-start | bytes 884744 | tf_op jit(solution)/shard_map/ppermute | solution.py:153
  10.1 12.5 %collective-permute-start.3 = (f32[4,48,384]{2,1,0:T(8,128)S(1)}, f32[4,48,384]{2,1,0:T(8,128)S(1)}, u32[]{:S(2)}, u32[]{:S(2)}) collective-permute-start(f32[4,48,384]{2,1,0:T(8,128)S(1)} %get-tuple-element.7), channel_id=1, source_target_pairs={{0,8},{4,12},{1,9},{5,13},{2,10},{6,14},{3,11},{7,15}} | collective-permute-start | bytes 884744 | tf_op jit(solution)/shard_map/ppermute | solution.py:153
  15.9 16.8 %collective-permute-start.14 = (f32[4,48,384]{2,1,0:T(8,128)S(1)}, f32[4,48,384]{2,1,0:T(8,128)S(1)}, u32[]{:S(2)}, u32[]{:S(2)}) collective-permute-start(f32[4,48,384]{2,1,0:T(8,128)S(1)} %collective-permute-done.12.refs_0_), channel_id=1, source_target_pairs={{0,4},{4,0},{8,12},{12,8},{16,20},{20,16},{24,28},{28,24},{1,5},{5... | collective-permute-start | bytes 884744 | tf_op jit(solution)/shard_map/ppermute | solution.py:133
  16.0 17.2 %collective-permute-start.15 = (f32[4,48,384]{2,1,0:T(8,128)S(1)}, f32[4,48,384]{2,1,0:T(8,128)S(1)}, u32[]{:S(2)}, u32[]{:S(2)}) collective-permute-start(f32[4,48,384]{2,1,0:T(8,128)S(1)} %collective-permute-done.13.refs_1_), channel_id=1, source_target_pairs={{0,4},{4,0},{8,12},{12,8},{16,20},{20,16},{24,28},{28,24},{1,5},{5... | collective-permute-start | bytes 884744 | tf_op jit(solution)/shard_map/ppermute | solution.py:133
  16.5 7.8 %collective-permute-start.6 = (f32[96,384]{1,0:T(8,128)S(1)}, f32[96,384]{1,0:T(8,128)S(1)}, u32[]{:S(2)}, u32[]{:S(2)}) collective-permute-start(f32[96,384]{1,0:T(8,128)S(1)} %bitcast.16), channel_id=1, source_target_pairs={{0,2},{1,3},{2,0},{3,1},{4,6},{5,7},{6,4},{7,5},{8,10},{9,11},{10,... | collective-permute-start | bytes 442376 | tf_op jit(solution)/shard_map/ppermute | solution.py:144
  22.2 5.9 %collective-permute-start.7 = (f32[96,384]{1,0:T(8,128)S(1)}, f32[96,384]{1,0:T(8,128)S(1)}, u32[]{:S(2)}, u32[]{:S(2)}) collective-permute-start(f32[96,384]{1,0:T(8,128)S(1)} %bitcast.17), channel_id=1, source_target_pairs={{0,3},{1,0},{2,1},{3,2},{4,7},{5,4},{6,5},{7,6},{8,11},{9,8},{10,9... | collective-permute-start | bytes 442376 | tf_op jit(solution)/shard_map/ppermute | solution.py:144
  22.6 10.1 %collective-permute-start.5 = (f32[96,384]{1,0:T(8,128)S(1)}, f32[96,384]{1,0:T(8,128)S(1)}, u32[]{:S(2)}, u32[]{:S(2)}) collective-permute-start(f32[96,384]{1,0:T(8,128)S(1)} %bitcast.18), channel_id=1, source_target_pairs={{0,1},{1,2},{2,3},{3,0},{4,5},{5,6},{6,7},{7,4},{8,9},{9,10},{10,1... | collective-permute-start | bytes 442376 | tf_op jit(solution)/shard_map/ppermute | solution.py:144
  24.3 13.6 %collective-permute-start.4 = (f32[4,48,384]{2,1,0:T(8,128)S(1)}, f32[4,48,384]{2,1,0:T(8,128)S(1)}, u32[]{:S(2)}, u32[]{:S(2)}) collective-permute-start(f32[4,48,384]{2,1,0:T(8,128)S(1)} %select_select_fusion.mine), channel_id=1, source_target_pairs={{0,4},{4,0},{8,12},{12,8},{16,20},{20,16},{24,28},{28,24},{1,5},{5... | collective-permute-start | bytes 884744 | tf_op jit(solution)/shard_map/ppermute | solution.py:133
  28.0 5.3 %collective-permute-start.8 = (f32[96,384]{1,0:T(8,128)S(1)}, f32[96,384]{1,0:T(8,128)S(1)}, u32[]{:S(2)}, u32[]{:S(2)}) collective-permute-start(f32[96,384]{1,0:T(8,128)S(1)} %bitcast.19), channel_id=1, source_target_pairs={{0,4},{4,0},{8,12},{12,8},{16,20},{20,16},{24,28},{28,24},{1,5},{5... | collective-permute-start | bytes 442376 | tf_op jit(solution)/shard_map/ppermute | solution.py:133
  32.7 1.4 %collective-permute-start.10 = (f32[96,384]{1,0:T(8,128)S(1)}, f32[96,384]{1,0:T(8,128)S(1)}, u32[]{:S(2)}, u32[]{:S(2)}) collective-permute-start(f32[96,384]{1,0:T(8,128)S(1)} %collective-permute-done.6.refs_2_), channel_id=1, source_target_pairs={{0,4},{4,0},{8,12},{12,8},{16,20},{20,16},{24,28},{28,24},{1,5},{5... | collective-permute-start | bytes 442376 | tf_op jit(solution)/shard_map/ppermute | solution.py:133
  32.7 1.6 %collective-permute-start.11 = (f32[96,384]{1,0:T(8,128)S(1)}, f32[96,384]{1,0:T(8,128)S(1)}, u32[]{:S(2)}, u32[]{:S(2)}) collective-permute-start(f32[96,384]{1,0:T(8,128)S(1)} %collective-permute-done.7.refs_3_), channel_id=1, source_target_pairs={{0,4},{4,0},{8,12},{12,8},{16,20},{20,16},{24,28},{28,24},{1,5},{5... | collective-permute-start | bytes 442376 | tf_op jit(solution)/shard_map/ppermute | solution.py:133
  33.2 1.4 %collective-permute-start.9 = (f32[96,384]{1,0:T(8,128)S(1)}, f32[96,384]{1,0:T(8,128)S(1)}, u32[]{:S(2)}, u32[]{:S(2)}) collective-permute-start(f32[96,384]{1,0:T(8,128)S(1)} %collective-permute-done.5.refs_1_), channel_id=1, source_target_pairs={{0,4},{4,0},{8,12},{12,8},{16,20},{20,16},{24,28},{28,24},{1,5},{5... | collective-permute-start | bytes 442376 | tf_op jit(solution)/shard_map/ppermute | solution.py:133
  38.9 9.6 %collective-permute-start.16 = (f32[48,384]{1,0:T(8,128)S(1)}, f32[48,384]{1,0:T(8,128)S(1)}, u32[]{:S(2)}, u32[]{:S(2)}) collective-permute-start(f32[48,384]{1,0:T(8,128)S(1)} %get-tuple-element.9), channel_id=1, source_target_pairs={{0,24},{4,28},{8,16},{12,20},{16,8},{20,12},{24,0},{28,4},{1,25},{... | collective-permute-start | bytes 221192 | tf_op jit(solution)/shard_map/ppermute | solution.py:176
  44.5 6.4 %collective-permute-start.17 = (f32[48,384]{1,0:T(8,128)S(1)}, f32[48,384]{1,0:T(8,128)S(1)}, u32[]{:S(2)}, u32[]{:S(2)}) collective-permute-start(f32[48,384]{1,0:T(8,128)S(1)} %get-tuple-element.11), channel_id=1, source_target_pairs={{0,16},{4,20},{8,24},{12,28},{16,0},{20,4},{24,8},{28,12},{1,17},{... | collective-permute-start | bytes 221192 | tf_op jit(solution)/shard_map/ppermute | solution.py:176
  48.5 4.4 %collective-permute-start.18 = (f32[48,384]{1,0:T(8,128)S(1)}, f32[48,384]{1,0:T(8,128)S(1)}, u32[]{:S(2)}, u32[]{:S(2)}) collective-permute-start(f32[48,384]{1,0:T(8,128)S(1)} %get-tuple-element.10), channel_id=1, source_target_pairs={{0,8},{4,12},{8,0},{12,4},{16,24},{20,28},{24,16},{28,20},{1,9},{5... | collective-permute-start | bytes 221192 | tf_op jit(solution)/shard_map/ppermute | solution.py:176

commit v3 on v2

--- a/solution.py
+++ b/solution.py
@@ -23,8 +23,9 @@
 
 def mul(left, right, right_dim=0):
     dims = (((1,), (right_dim,)), ((), ()))
-    dot = functools.partial(lax.dot_general, dimension_numbers=dims, preferred_element_type=F32)
-    return dot(left[0], right[0]) + (dot(left[0], right[1]) + dot(left[1], right[0]))
+    lefts = jnp.concatenate([left[0], left[1], left[0]], 1)
+    rights = jnp.concatenate([right[0], right[0], right[1]], right_dim)
+    return lax.dot_general(lefts, rights, dims, preferred_element_type=F32)
 
 
 def call(kernel, outs, operands, scratch=(), flops=0):
@@ -40,6 +41,10 @@
     )(*operands)
 
 
+def load_kernel(own, copy):
+    copy[...] = own[...]
+
+
 def pair_kernel(own, other, half, even_t, work):
     core = lax.rem(lax.axis_index("tm"), 2)
     chips, rows, order_dim = half.shape
@@ -61,22 +66,16 @@
     whole[:, 1 - core] = theirs[...]
 
 
-def chain_kernel(chips, *refs):
-    count = chips - 2
-    mine, theirs, (out, whole) = refs[:count], refs[count : 2 * count], refs[2 * count :]
-    place = lax.axis_index("tm")
-    chip, core = place // 2, lax.rem(place, 2)
-    order_dim = out.shape[0]
-    for shift in range(1, chips - 1):
-
-        @pl.when(chip > shift)
-        def _(shift=shift):
-            fill(whole, core, mine[shift - 1], theirs[shift - 1])
-            step = whole[...].reshape(order_dim, order_dim)
-            if shift == 1:
-                out[...] = step
-            else:
-                out[...] = mul(parts(step), parts(out[...]))
+def chain_kernel(near, near_other, across, across_other, out, whole):
+    place = lax.axis_index("tm")
+    chip, core = place // 2, lax.rem(place, 2)
+
+    @pl.when(chip == 3)
+    def _():
+        fill(whole, core, across, across_other)
+        left = parts(whole[...].reshape(out.shape))
+        fill(whole, core, near, near_other)
+        out[...] = mul(left, parts(whole[...].reshape(out.shape)))
 
 
 def local_kernel(planes, *refs):
@@ -92,33 +91,61 @@
     left = parts(even_t[...])
     total = both[0] + mul(parts(mul(left, parts(both[1]))), left, 1)
 
-    @pl.when(chip < 2)
+    @pl.when(chip < 3)
     def _():
         out[...] = total
 
-    @pl.when(chip >= 2)
+    @pl.when(chip == 3)
     def _():
         left = parts(chain[...])
         out[...] = mul(parts(mul(left, parts(total))), left, 1)
 
 
-def last_kernel(mine, theirs, total, out, whole):
-    place = lax.axis_index("tm")
-    chip, core = place // 2, lax.rem(place, 2)
-    order_dim = total.shape[0]
-    chips, rows = out.shape[:2]
+def left_kernel(near, far, total, out):
+    place = lax.axis_index("tm")
+    chip, core = place // 2, lax.rem(place, 2)
+    chips, rows, order_dim = out.shape
 
     @pl.when(chip == 0)
     def _():
         for k in range(chips):
             out[k] = total[pl.ds(pl.multiple_of((2 * k + core) * rows, 8), rows), :]
 
-    @pl.when(chip > 0)
-    def _():
+    def run(mine):
+        left = parts(mine[...].reshape(chips * rows, order_dim))
+        out[...] = mul(left, parts(total[...])).reshape(out.shape)
+
+    pl.when(chip == 1)(lambda: run(near))
+    pl.when(chip == 3)(lambda: run(far))
+
+
+def right_kernel(near, near_other, across, across_other, far, far_other, left, total, out, whole):
+    place = lax.axis_index("tm")
+    chip, core = place // 2, lax.rem(place, 2)
+    chips, rows, order_dim = out.shape
+    tall, square = (chips * rows, order_dim), total.shape
+
+    @pl.when(chip == 0)
+    def _():
+        out[...] = left[...]
+
+    def run(mine, theirs):
         fill(whole, core, mine, theirs)
-        right = parts(whole[...].reshape(order_dim, order_dim))
-        left = parts(mine[...].reshape(order_dim // 2, order_dim))
-        out[...] = mul(parts(mul(left, parts(total[...]))), right, 1).reshape(out.shape)
+        right = parts(whole[...].reshape(square))
+        out[...] = mul(parts(left[...].reshape(tall)), right, 1).reshape(out.shape)
+
+    pl.when(chip == 1)(lambda: run(near, near_other))
+    pl.when(chip == 3)(lambda: run(far, far_other))
+
+    @pl.when(chip == 2)
+    def _():
+        fill(whole, core, far, far_other)
+        right = parts(whole[...].reshape(square))
+        value = mul(parts(across[...].reshape(tall)), right)
+        value = mul(parts(mul(parts(value), parts(total[...]))), right, 1)
+        fill(whole, core, across, across_other)
+        right = parts(whole[...].reshape(square))
+        out[...] = mul(parts(value), right, 1).reshape(out.shape)
 
 
 def body(propagators, perturbation):
@@ -127,14 +154,11 @@
     chips = devices // 2
     order_dim = propagators.shape[1]
     out_rows = order_dim // devices
-    place = lax.axis_index("tm")
-    chip = place // 2
-    partner = [(i, i ^ 1) for i in range(devices)]
-    swap = lambda x: lax.ppermute(x, "tm", partner)
+    chip = lax.axis_index("tm") // 2
+    swap = lambda x: lax.ppermute(x, "tm", [(i, i ^ 1) for i in range(devices)])
     cube = 2 * order_dim**3
-
-    def chip_pairs(pairs):
-        return [(2 * i + c, 2 * j + c) for i, j in pairs for c in range(2)]
+    half_shape = (chips, out_rows, order_dim)
+    whole_shape = (chips, 2, out_rows, order_dim)
 
     own = propagators[0]
     rows = perturbation[0]
@@ -142,38 +166,30 @@
     blocks = [rows]
     for shift in range(1, planes):
         blocks.append(lax.ppermute(rows, "group", [(i, (i + shift) % planes) for i in range(planes)]))
-    half_shape = (chips, out_rows, order_dim)
+    (own,) = call(load_kernel, [own.shape], [own])
     half, even_t = call(pair_kernel, [half_shape, own.shape], [own, other], [half_shape], 2 * cube)
 
-    sent = []
-    for shift in range(1, chips - 1):
-        sent.append(lax.ppermute(half, "tm", chip_pairs([(i, i + shift) for i in range(1, chips - shift)])))
-    first = []
-    for shift in range(1, chips):
-        first.append(lax.ppermute(half, "tm", chip_pairs([(0, shift)])))
-    sent_other = []
-    for shift in range(1, chips - 1):
-        sent_other.append(swap(sent[shift - 1]))
-    (chain,) = call(
-        functools.partial(chain_kernel, chips), [own.shape], sent + sent_other,
-        [(chips, 2, out_rows, order_dim)], 3 * cube,
-    )
+    mine, theirs = {}, {}
+    for way in (2, 1, 3):
+        pairs = [(i, i ^ (2 * way)) for i in range(devices) if i < i ^ (2 * way)]
+        mine[way] = lax.ppermute(half, "tm", pairs)
+    for way in (2, 1, 3):
+        theirs[way] = swap(mine[way])
+    operands = [mine[1], theirs[1], mine[2], theirs[2]]
+    (chain,) = call(chain_kernel, [own.shape], operands, [whole_shape], 2 * cube)
     blocks_other = []
     for shift in range(planes):
         blocks_other.append(swap(blocks[shift]))
-    (total,) = call(
-        functools.partial(local_kernel, planes), [own.shape],
-        blocks + blocks_other + [even_t, chain], [(2,) + own.shape], 12 * cube,
-    )
-    mine = first[0]
-    for shift in range(2, chips):
-        mine = jnp.where(chip == shift, first[shift - 1], mine)
-    theirs = swap(mine)
-    (terms,) = call(last_kernel, [half_shape], [mine, theirs, total], [(chips, 2, out_rows, order_dim)], 3 * cube)
+    operands = blocks + blocks_other + [even_t, chain]
+    kernel = functools.partial(local_kernel, planes)
+    (total,) = call(kernel, [own.shape], operands, [(2,) + own.shape], 12 * cube)
+    (left,) = call(left_kernel, [half_shape], [mine[1], mine[3], total], [], 2 * cube)
+    operands = [x[way] for way in (1, 2, 3) for x in (mine, theirs)] + [left, total]
+    (terms,) = call(right_kernel, [half_shape], operands, [whole_shape], 2 * cube)
     out = lax.dynamic_index_in_dim(terms, chip, 0, False)
-    for shift in range(chips - 1, 0, -1):
-        block = lax.dynamic_index_in_dim(terms, chip ^ shift, 0, False)
-        out = out + lax.ppermute(block, "tm", [(i, i ^ (2 * shift)) for i in range(devices)])
+    for way in (3, 2, 1):
+        block = lax.dynamic_index_in_dim(terms, chip ^ way, 0, False)
+        out = out + lax.ppermute(block, "tm", [(i, i ^ (2 * way)) for i in range(devices)])
     return out
 
 
@@ -231,8 +247,7 @@
     def step(propagators, perturbation):
         order_dim = propagators.shape[1]
         tiled = order_dim // planes % 8 == 0 and order_dim // (2 * chips) % 8 == 0
-        power = chips & (chips - 1) == 0 and chips > 2
-        plan = body if tiled and power else plain_body
+        plan = body if tiled and chips == 4 else plain_body
         return jax.shard_map(plan, mesh=mesh, in_specs=in_specs, out_specs=out_specs, check_vma=False)(
             propagators, perturbation
         )

time: 53.8 us -> 49.9 us (0.928)
  the two profiles are of different devices: /device:TPU:20 before, /device:TPU:24 now
where the time goes in v3:
time: 49.9 us; the launch traced here: 49.7 us
  waiting for transfers between devices  29.7 us (60%)
  starting transfers between devices  16 us (32%)
  Pallas kernels  2.15 us (4%)
  local copies, waits for them, and re-layouts  1.1 us (2%)
  other arithmetic  0.65 us (1%)
    ppermute x3, waiting for transfers between devices, body(): lax.ppermute(rows, 'group', [(i, (i + shift) % planes) for i in range(pla...  12.6 us
    ppermute x3, waiting for transfers between devices, body(): mine[way] = lax.ppermute(half, 'tm', pairs)  11 us
    ppermute x3, starting transfers between devices, body(): mine[way] = lax.ppermute(half, 'tm', pairs)  8.16 us
    ppermute x3, starting transfers between devices, body(): lax.ppermute(block, 'tm', [(i, i ^ 2 * way) for i in range(devices)])  5.7 us
    ppermute x3, waiting for transfers between devices, body(): lax.ppermute(block, 'tm', [(i, i ^ 2 * way) for i in range(devices)])  4.02 us
    pallas_call x6, Pallas kernels, call(): pl.pallas_call(kernel, out_shape=outs, in_specs=[VMEM] * len(operands), o...  2.15 us
    ppermute x8, waiting for transfers between devices, body(): swap = lambda x: lax.ppermute(x, 'tm', [(i, i ^ 1) for i in range(devices)])  2.09 us
    ppermute x8, starting transfers between devices, body(): swap = lambda x: lax.ppermute(x, 'tm', [(i, i ^ 1) for i in range(devices)])  1.1 us
  transfers between devices with their start and end apart: 17, of which 11 were waited for; matrix products, arithmetic and copies ran while one was open for 0% of the time, Pallas kernels for 3%

profile of v3, /device:TPU:24, one launch (start us, length us, event | category | flops | bytes accessed | tf_op | source)
XLA Modules:
  0.0 49.7 jit_solution(201550924866712815)
XLA Ops:
  0.0 0.0 collective-permute-start
  0.0 0.0 copy-start
  0.0 1.1 %copy-done = f32[1,384,384]{2,1,0:T(8,128)S(1)} copy-done((f32[1,384,384]{2,1,0:T(8,128)S(1)}, f32[1,384,384]{2,1,0:T(8,128)}, u32[]{:S(2)}) %copy-start) | copy-done | bytes 589848
  1.1 0.0 copy-start.1
  1.1 1.1 %collective-permute-done.other = f32[384,384]{1,0:T(8,128)S(1)} collective-permute-done((f32[384,384]{1,0:T(8,128)}, f32[384,384]{1,0:T(8,128)S(1)}, u32[]{:S(2)}, u32[]{:S(2)}) %collective-permute-start) | collective-permute-done | bytes 589856 | tf_op jit(solution)/shard_map/ppermute | solution.py:158
  2.2 0.7 %shard_map.29 = (f32[4,48,384]{2,1,0:T(8,128)S(1)}, f32[384,384]{1,0:T(8,128)S(1)}) custom-call(f32[384,384]{1,0:T(8,128)S(1)} %shard_map.28.own, f32[384,384]{1,0:T(8,128)S(1)} %collective-permute-done.other), custom_call_target="tpu_custom_call" | custom-call | flops 226492416 | tf_op jit(solution)/shard_map/pallas_call | solution.py:33
  2.9 3.4 %collective-permute-start.1 = (f32[4,48,384]{2,1,0:T(8,128)S(1)}, f32[4,48,384]{2,1,0:T(8,128)S(1)}, u32[]{:S(2)}, u32[]{:S(2)}) collective-permute-start(f32[4,48,384]{2,1,0:T(8,128)S(1)} %get-tuple-element.7), channel_id=1, source_target_pairs={{0,8},{4,12},{16,24},{20,28},{1,9},{5,13},{17,25},{21,29},{2,10},{... | collective-permute-start | bytes 884744 | tf_op jit(solution)/shard_map/ppermute | solution.py:175
  6.3 3.4 %collective-permute-start.3 = (f32[4,48,384]{2,1,0:T(8,128)S(1)}, f32[4,48,384]{2,1,0:T(8,128)S(1)}, u32[]{:S(2)}, u32[]{:S(2)}) collective-permute-start(f32[4,48,384]{2,1,0:T(8,128)S(1)} %get-tuple-element.7), channel_id=1, source_target_pairs={{0,16},{4,20},{8,24},{12,28},{1,17},{5,21},{9,25},{13,29},{2,18},{... | collective-permute-start | bytes 884744 | tf_op jit(solution)/shard_map/ppermute | solution.py:175
  9.8 0.0 copy-done.1
  9.8 0.3 collective-permute-start.7
  10.0 1.3 %collective-permute-start.5 = (f32[4,48,384]{2,1,0:T(8,128)S(1)}, f32[4,48,384]{2,1,0:T(8,128)S(1)}, u32[]{:S(2)}, u32[]{:S(2)}) collective-permute-start(f32[4,48,384]{2,1,0:T(8,128)S(1)} %get-tuple-element.7), channel_id=1, source_target_pairs={{0,24},{4,28},{8,16},{12,20},{1,25},{5,29},{9,17},{13,21},{2,26},{... | collective-permute-start | bytes 884744 | tf_op jit(solution)/shard_map/ppermute | solution.py:175
  11.4 2.3 %collective-permute-done.1.near = f32[4,48,384]{2,1,0:T(8,128)S(1)} collective-permute-done((f32[4,48,384]{2,1,0:T(8,128)S(1)}, f32[4,48,384]{2,1,0:T(8,128)S(1)}, u32[]{:S(2)}, u32[]{:S(2)}) %collective-permute-start.1) | collective-permute-done | bytes 294944 | tf_op jit(solution)/shard_map/ppermute | solution.py:175
  13.7 0.0 collective-permute-start.2
  13.7 8.6 %collective-permute-done.3.across = f32[4,48,384]{2,1,0:T(8,128)S(1)} collective-permute-done((f32[4,48,384]{2,1,0:T(8,128)S(1)}, f32[4,48,384]{2,1,0:T(8,128)S(1)}, u32[]{:S(2)}, u32[]{:S(2)}) %collective-permute-start.3) | collective-permute-done | bytes 294944 | tf_op jit(solution)/shard_map/ppermute | solution.py:175
  22.3 0.0 collective-permute-start.4
  22.3 0.3 collective-permute-start.8
  22.7 0.0 collective-permute-done.7.refs_1_
  22.7 0.4 collective-permute-start.9
  23.1 12.6 %collective-permute-done.8.refs_2_ = f32[96,384]{1,0:T(8,128)S(1)} collective-permute-done((f32[96,384]{1,0:T(8,128)S(1)}, f32[96,384]{1,0:T(8,128)S(1)}, u32[]{:S(2)}, u32[]{:S(2)}) %collective-permute-start.8) | collective-permute-done | bytes 147488 | tf_op jit(solution)/shard_map/ppermute | solution.py:168
  35.7 0.1 collective-permute-start.10
  35.8 0.0 collective-permute-done.9.refs_3_
  35.8 0.4 collective-permute-start.11
  36.2 0.0 collective-permute-done.5.far
  36.2 0.1 collective-permute-start.12
  36.3 0.0 collective-permute-done.2.near_other
  36.3 0.4 collective-permute-start.13
  36.7 0.0 collective-permute-done.4.across_other
  36.7 0.1 collective-permute-start.6
  36.8 0.3 collective-permute-done.10.refs_4_
  37.1 0.2 collective-permute-done.11.refs_5_
  37.3 0.3 collective-permute-done.12.refs_6_
  37.6 0.2 collective-permute-done.13.refs_7_
  37.8 1.4 %shard_map.31.total = f32[384,384]{1,0:T(8,128)S(1)} custom-call(f32[96,384]{1,0:T(8,128)S(1)} %bitcast.20, f32[96,384]{1,0:T(8,128)S(1)} %collective-permute-done.7.refs_1_, f32[96,384]{1,0:T(8,128)S(1)} %collective-permute-done.8.refs_2_, f32[96,384]{1,0:T(8,128)S(1)} %collective-permute-done.9.refs_3_, f32[96,384]{1,0:T(8,128)S(1)} %collective-permute-done.10.refs_4_, ...), custom_call_target="tpu_custom_call" | custom-call | flops 1358954496 | tf_op jit(solution)/shard_map/pallas_call | solution.py:33
  39.2 0.1 shard_map.32.left
  39.2 0.0 collective-permute-done.6.far_other
  39.2 0.1 shard_map.33
  39.3 3.7 %collective-permute-start.14 = (f32[48,384]{1,0:T(8,128)S(1)}, f32[48,384]{1,0:T(8,128)S(1)}, u32[]{:S(2)}, u32[]{:S(2)}) collective-permute-start(f32[48,384]{1,0:T(8,128)S(1)} %get-tuple-element.9), channel_id=1, source_target_pairs={{0,24},{4,28},{8,16},{12,20},{16,8},{20,12},{24,0},{28,4},{1,25},{... | collective-permute-start | bytes 221192 | tf_op jit(solution)/shard_map/ppermute | solution.py:192
  43.0 0.6 %collective-permute-start.15 = (f32[48,384]{1,0:T(8,128)S(1)}, f32[48,384]{1,0:T(8,128)S(1)}, u32[]{:S(2)}, u32[]{:S(2)}) collective-permute-start(f32[48,384]{1,0:T(8,128)S(1)} %get-tuple-element.11), channel_id=1, source_target_pairs={{0,16},{4,20},{8,24},{12,28},{16,0},{20,4},{24,8},{28,12},{1,17},{... | collective-permute-start | bytes 221192 | tf_op jit(solution)/shard_map/ppermute | solution.py:192
  43.6 1.4 %collective-permute-start.16 = (f32[48,384]{1,0:T(8,128)S(1)}, f32[48,384]{1,0:T(8,128)S(1)}, u32[]{:S(2)}, u32[]{:S(2)}) collective-permute-start(f32[48,384]{1,0:T(8,128)S(1)} %get-tuple-element.10), channel_id=1, source_target_pairs={{0,8},{4,12},{8,0},{12,4},{16,24},{20,28},{24,16},{28,20},{1,9},{5... | collective-permute-start | bytes 221192 | tf_op jit(solution)/shard_map/ppermute | solution.py:192
  45.0 0.8 %collective-permute-done.14 = f32[48,384]{1,0:T(8,128)S(1)} collective-permute-done((f32[48,384]{1,0:T(8,128)S(1)}, f32[48,384]{1,0:T(8,128)S(1)}, u32[]{:S(2)}, u32[]{:S(2)}) %collective-permute-start.14) | collective-permute-done | bytes 73760 | tf_op jit(solution)/shard_map/ppermute | solution.py:192
  45.8 1.6 %collective-permute-done.15 = f32[48,384]{1,0:T(8,128)S(1)} collective-permute-done((f32[48,384]{1,0:T(8,128)S(1)}, f32[48,384]{1,0:T(8,128)S(1)}, u32[]{:S(2)}, u32[]{:S(2)}) %collective-permute-start.15) | collective-permute-done | bytes 73760 | tf_op jit(solution)/shard_map/ppermute | solution.py:192
  47.4 1.7 %collective-permute-done.16 = f32[48,384]{1,0:T(8,128)S(1)} collective-permute-done((f32[48,384]{1,0:T(8,128)S(1)}, f32[48,384]{1,0:T(8,128)S(1)}, u32[]{:S(2)}, u32[]{:S(2)}) %collective-permute-start.16) | collective-permute-done | bytes 73760 | tf_op jit(solution)/shard_map/ppermute | solution.py:192
  49.0 0.7 %fusion.1 = f32[48,384]{1,0:T(8,128)} fusion(f32[48,384]{1,0:T(8,128)S(1)} %collective-permute-done.16, f32[48,384]{1,0:T(8,128)S(1)} %collective-permute-done.15, f32[48,384]{1,0:T(8,128)S(1)} %collective-permute-done.14, f32[4,48,384]{2,1,0:T(8,128)S(1)} %shard_map.33, s32[]{:T(128)S(6)} %select_n.19), kind=kLoop, calls=%fused_computation.2 | loop fusion | flops 55296 | bytes 368644 | tf_op jit(solution)/shard_map/add | solution.py:192
  (3 shorter events, 0.1 us)
Async XLA Ops:
  0.0 2.2 %collective-permute-start = (f32[384,384]{1,0:T(8,128)}, f32[384,384]{1,0:T(8,128)S(1)}, u32[]{:S(2)}, u32[]{:S(2)}) collective-permute-start(f32[384,384]{1,0:T(8,128)} %bitcast.14), channel_id=1, source_target_pairs={{0,4},{4,0},{8,12},{12,8},{16,20},{20,16},{24,28},{28,24},{1,5},{5... | collective-permute-start | bytes 1769480 | tf_op jit(solution)/shard_map/ppermute | solution.py:158
  0.0 1.1 %copy-start = (f32[1,384,384]{2,1,0:T(8,128)S(1)}, f32[1,384,384]{2,1,0:T(8,128)}, u32[]{:S(2)}) copy-start(f32[1,384,384]{2,1,0:T(8,128)} %param.2) | copy-start | bytes 1769476
  1.1 8.6 %copy-start.1 = (f32[1,96,384]{2,1,0:T(8,128)S(1)}, f32[1,96,384]{2,1,0:T(8,128)}, u32[]{:S(2)}) copy-start(f32[1,96,384]{2,1,0:T(8,128)} %param.3) | copy-start | bytes 442372
  2.9 10.8 %collective-permute-start.1 = (f32[4,48,384]{2,1,0:T(8,128)S(1)}, f32[4,48,384]{2,1,0:T(8,128)S(1)}, u32[]{:S(2)}, u32[]{:S(2)}) collective-permute-start(f32[4,48,384]{2,1,0:T(8,128)S(1)} %get-tuple-element.7), channel_id=1, source_target_pairs={{0,8},{4,12},{16,24},{20,28},{1,9},{5,13},{17,25},{21,29},{2,10},{... | collective-permute-start | bytes 884744 | tf_op jit(solution)/shard_map/ppermute | solution.py:175
  6.3 16.0 %collective-permute-start.3 = (f32[4,48,384]{2,1,0:T(8,128)S(1)}, f32[4,48,384]{2,1,0:T(8,128)S(1)}, u32[]{:S(2)}, u32[]{:S(2)}) collective-permute-start(f32[4,48,384]{2,1,0:T(8,128)S(1)} %get-tuple-element.7), channel_id=1, source_target_pairs={{0,16},{4,20},{8,24},{12,28},{1,17},{5,21},{9,25},{13,29},{2,18},{... | collective-permute-start | bytes 884744 | tf_op jit(solution)/shard_map/ppermute | solution.py:175
  9.8 12.9 %collective-permute-start.7 = (f32[96,384]{1,0:T(8,128)S(1)}, f32[96,384]{1,0:T(8,128)S(1)}, u32[]{:S(2)}, u32[]{:S(2)}) collective-permute-start(f32[96,384]{1,0:T(8,128)S(1)} %bitcast.16), channel_id=1, source_target_pairs={{0,1},{1,2},{2,3},{3,0},{4,5},{5,6},{6,7},{7,4},{8,9},{9,10},{10,1... | collective-permute-start | bytes 442376 | tf_op jit(solution)/shard_map/ppermute | solution.py:168
  10.0 26.2 %collective-permute-start.5 = (f32[4,48,384]{2,1,0:T(8,128)S(1)}, f32[4,48,384]{2,1,0:T(8,128)S(1)}, u32[]{:S(2)}, u32[]{:S(2)}) collective-permute-start(f32[4,48,384]{2,1,0:T(8,128)S(1)} %get-tuple-element.7), channel_id=1, source_target_pairs={{0,24},{4,28},{8,16},{12,20},{1,25},{5,29},{9,17},{13,21},{2,26},{... | collective-permute-start | bytes 884744 | tf_op jit(solution)/shard_map/ppermute | solution.py:175
  13.7 22.6 %collective-permute-start.2 = (f32[4,48,384]{2,1,0:T(8,128)S(1)}, f32[4,48,384]{2,1,0:T(8,128)S(1)}, u32[]{:S(2)}, u32[]{:S(2)}) collective-permute-start(f32[4,48,384]{2,1,0:T(8,128)S(1)} %collective-permute-done.1.near), channel_id=1, source_target_pairs={{0,4},{4,0},{8,12},{12,8},{16,20},{20,16},{24,28},{28,24},{1,5},{5... | collective-permute-start | bytes 884744 | tf_op jit(solution)/shard_map/ppermute | solution.py:158
  22.3 14.4 %collective-permute-start.4 = (f32[4,48,384]{2,1,0:T(8,128)S(1)}, f32[4,48,384]{2,1,0:T(8,128)S(1)}, u32[]{:S(2)}, u32[]{:S(2)}) collective-permute-start(f32[4,48,384]{2,1,0:T(8,128)S(1)} %collective-permute-done.3.across), channel_id=1, source_target_pairs={{0,4},{4,0},{8,12},{12,8},{16,20},{20,16},{24,28},{28,24},{1,5},{5... | collective-permute-start | bytes 884744 | tf_op jit(solution)/shard_map/ppermute | solution.py:158
  22.3 13.4 %collective-permute-start.8 = (f32[96,384]{1,0:T(8,128)S(1)}, f32[96,384]{1,0:T(8,128)S(1)}, u32[]{:S(2)}, u32[]{:S(2)}) collective-permute-start(f32[96,384]{1,0:T(8,128)S(1)} %bitcast.17), channel_id=1, source_target_pairs={{0,2},{1,3},{2,0},{3,1},{4,6},{5,7},{6,4},{7,5},{8,10},{9,11},{10,... | collective-permute-start | bytes 442376 | tf_op jit(solution)/shard_map/ppermute | solution.py:168
  22.7 13.1 %collective-permute-start.9 = (f32[96,384]{1,0:T(8,128)S(1)}, f32[96,384]{1,0:T(8,128)S(1)}, u32[]{:S(2)}, u32[]{:S(2)}) collective-permute-start(f32[96,384]{1,0:T(8,128)S(1)} %bitcast.18), channel_id=1, source_target_pairs={{0,3},{1,0},{2,1},{3,2},{4,7},{5,4},{6,5},{7,6},{8,11},{9,8},{10,9... | collective-permute-start | bytes 442376 | tf_op jit(solution)/shard_map/ppermute | solution.py:168
  35.7 1.4 %collective-permute-start.10 = (f32[96,384]{1,0:T(8,128)S(1)}, f32[96,384]{1,0:T(8,128)S(1)}, u32[]{:S(2)}, u32[]{:S(2)}) collective-permute-start(f32[96,384]{1,0:T(8,128)S(1)} %bitcast.19), channel_id=1, source_target_pairs={{0,4},{4,0},{8,12},{12,8},{16,20},{20,16},{24,28},{28,24},{1,5},{5... | collective-permute-start | bytes 442376 | tf_op jit(solution)/shard_map/ppermute | solution.py:158
  35.8 1.5 %collective-permute-start.11 = (f32[96,384]{1,0:T(8,128)S(1)}, f32[96,384]{1,0:T(8,128)S(1)}, u32[]{:S(2)}, u32[]{:S(2)}) collective-permute-start(f32[96,384]{1,0:T(8,128)S(1)} %collective-permute-done.7.refs_1_), channel_id=1, source_target_pairs={{0,4},{4,0},{8,12},{12,8},{16,20},{20,16},{24,28},{28,24},{1,5},{5... | collective-permute-start | bytes 442376 | tf_op jit(solution)/shard_map/ppermute | solution.py:158
  36.2 1.4 %collective-permute-start.12 = (f32[96,384]{1,0:T(8,128)S(1)}, f32[96,384]{1,0:T(8,128)S(1)}, u32[]{:S(2)}, u32[]{:S(2)}) collective-permute-start(f32[96,384]{1,0:T(8,128)S(1)} %collective-permute-done.8.refs_2_), channel_id=1, source_target_pairs={{0,4},{4,0},{8,12},{12,8},{16,20},{20,16},{24,28},{28,24},{1,5},{5... | collective-permute-start | bytes 442376 | tf_op jit(solution)/shard_map/ppermute | solution.py:158
  36.3 1.5 %collective-permute-start.13 = (f32[96,384]{1,0:T(8,128)S(1)}, f32[96,384]{1,0:T(8,128)S(1)}, u32[]{:S(2)}, u32[]{:S(2)}) collective-permute-start(f32[96,384]{1,0:T(8,128)S(1)} %collective-permute-done.9.refs_3_), channel_id=1, source_target_pairs={{0,4},{4,0},{8,12},{12,8},{16,20},{20,16},{24,28},{28,24},{1,5},{5... | collective-permute-start | bytes 442376 | tf_op jit(solution)/shard_map/ppermute | solution.py:158
  36.7 2.5 %collective-permute-start.6 = (f32[4,48,384]{2,1,0:T(8,128)S(1)}, f32[4,48,384]{2,1,0:T(8,128)S(1)}, u32[]{:S(2)}, u32[]{:S(2)}) collective-permute-start(f32[4,48,384]{2,1,0:T(8,128)S(1)} %collective-permute-done.5.far), channel_id=1, source_target_pairs={{0,4},{4,0},{8,12},{12,8},{16,20},{20,16},{24,28},{28,24},{1,5},{5... | collective-permute-start | bytes 884744 | tf_op jit(solution)/shard_map/ppermute | solution.py:158
  39.3 6.5 %collective-permute-start.14 = (f32[48,384]{1,0:T(8,128)S(1)}, f32[48,384]{1,0:T(8,128)S(1)}, u32[]{:S(2)}, u32[]{:S(2)}) collective-permute-start(f32[48,384]{1,0:T(8,128)S(1)} %get-tuple-element.9), channel_id=1, source_target_pairs={{0,24},{4,28},{8,16},{12,20},{16,8},{20,12},{24,0},{28,4},{1,25},{... | collective-permute-start | bytes 221192 | tf_op jit(solution)/shard_map/ppermute | solution.py:192
  43.0 4.4 %collective-permute-start.15 = (f32[48,384]{1,0:T(8,128)S(1)}, f32[48,384]{1,0:T(8,128)S(1)}, u32[]{:S(2)}, u32[]{:S(2)}) collective-permute-start(f32[48,384]{1,0:T(8,128)S(1)} %get-tuple-element.11), channel_id=1, source_target_pairs={{0,16},{4,20},{8,24},{12,28},{16,0},{20,4},{24,8},{28,12},{1,17},{... | collective-permute-start | bytes 221192 | tf_op jit(solution)/shard_map/ppermute | solution.py:192
  43.6 5.4 %collective-permute-start.16 = (f32[48,384]{1,0:T(8,128)S(1)}, f32[48,384]{1,0:T(8,128)S(1)}, u32[]{:S(2)}, u32[]{:S(2)}) collective-permute-start(f32[48,384]{1,0:T(8,128)S(1)} %get-tuple-element.10), channel_id=1, source_target_pairs={{0,8},{4,12},{8,0},{12,4},{16,24},{20,28},{24,16},{28,20},{1,9},{5... | collective-permute-start | bytes 221192 | tf_op jit(solution)/shard_map/ppermute | solution.py:192

commit v4 on v3

--- a/solution.py
+++ b/solution.py
@@ -1,5 +1,3 @@
-import functools
-
 import jax
 import jax.numpy as jnp
 from jax import lax
@@ -41,8 +39,18 @@
     )(*operands)
 
 
-def load_kernel(own, copy):
+def load_kernel(own, rows, copy, part):
+    plane = lax.axis_index("group")
+    lanes = part.shape[1]
     copy[...] = own[...]
+
+    @pl.when(plane < 2)
+    def _():
+        part[...] = rows[:, :lanes]
+
+    @pl.when(plane >= 2)
+    def _():
+        part[...] = rows[:, lanes // 2 :]
 
 
 def pair_kernel(own, other, half, even_t, work):
@@ -66,86 +74,109 @@
     whole[:, 1 - core] = theirs[...]
 
 
-def chain_kernel(near, near_other, across, across_other, out, whole):
-    place = lax.axis_index("tm")
-    chip, core = place // 2, lax.rem(place, 2)
+def carry_kernel(even_t, step, step_other, skip, skip_other, out, whole):
+    place = lax.axis_index("tm")
+    chip, core = place // 2, lax.rem(place, 2)
+    shape = out.shape
+
+    @pl.when((chip < 2) & (core == 1))
+    def _():
+        out[...] = even_t[...]
+
+    @pl.when(chip >= 2)
+    def _():
+        fill(whole, core, step, step_other)
+        out[...] = whole[...].reshape(shape)
 
     @pl.when(chip == 3)
     def _():
-        fill(whole, core, across, across_other)
-        left = parts(whole[...].reshape(out.shape))
-        fill(whole, core, near, near_other)
-        out[...] = mul(left, parts(whole[...].reshape(out.shape)))
-
-
-def local_kernel(planes, *refs):
-    mine, theirs = refs[:planes], refs[planes : 2 * planes]
-    even_t, chain, out, both = refs[2 * planes :]
+        fill(whole, core, skip, skip_other)
+        out[...] = mul(parts(whole[...].reshape(shape)), parts(out[...]))
+
+    @pl.when((chip >= 2) & (core == 1))
+    def _():
+        out[...] = mul(parts(out[...]), parts(even_t[...]))
+
+
+def local_kernel(rows, beside, skip, cross, carry, out, full):
     place, plane = lax.axis_index("tm"), lax.axis_index("group")
     chip, core = place // 2, lax.rem(place, 2)
-    rows = mine[0].shape[0]
-    for shift in range(planes):
-        start = pl.multiple_of(lax.rem(plane + planes - shift, planes) * rows, 8)
-        both[core, pl.ds(start, rows), :] = mine[shift][...]
-        both[1 - core, pl.ds(start, rows), :] = theirs[shift][...]
-    left = parts(even_t[...])
-    total = both[0] + mul(parts(mul(left, parts(both[1]))), left, 1)
-
-    @pl.when(chip < 3)
-    def _():
-        out[...] = total
-
-    @pl.when(chip == 3)
-    def _():
-        left = parts(chain[...])
-        out[...] = mul(parts(mul(left, parts(total))), left, 1)
-
-
-def left_kernel(near, far, total, out):
+    count, lanes = rows.shape[0], skip.shape[1]
+    next_to = plane + 1 - 2 * lax.rem(plane, 2)
+
+    def at(block):
+        return pl.ds(pl.multiple_of(block * count, 8), count)
+
+    full[at(plane), :] = rows[...]
+    full[at(next_to), :] = beside[...]
+
+    @pl.when(plane < 2)
+    def _():
+        full[at(plane + 2), lanes // 2 :] = skip[...]
+        full[at(3 - plane), lanes // 2 :] = cross[...]
+
+    @pl.when(plane >= 2)
+    def _():
+        full[at(plane - 2), :lanes] = skip[...]
+        full[at(3 - plane), :lanes] = cross[...]
+
+    row = lax.broadcasted_iota(jnp.int32, full.shape, 0)
+    lane = lax.broadcasted_iota(jnp.int32, full.shape, 1)
+    low = (row < 2 * count) & (lane < jnp.where(plane < 2, 2 * lanes, lanes))
+    high = (row >= 2 * count) & (lane >= jnp.where(plane < 2, lanes // 2, 0))
+    value = jnp.where(low | high, full[...], full[...].T)
+    plain = (chip < 2) & (core == 0)
+
+    @pl.when(plain)
+    def _():
+        out[...] = value
+
+    @pl.when(jnp.logical_not(plain))
+    def _():
+        left = parts(carry[...])
+        out[...] = mul(parts(mul(left, parts(value))), left, 1)
+
+
+def pick_kernel(first, second, third, out):
+    chip = lax.axis_index("tm") // 2
+    for k, half in ((1, first), (2, second), (3, third)):
+
+        @pl.when(chip == k)
+        def _(half=half):
+            out[...] = half[...]
+
+
+def left_kernel(mine, one, two, out, total):
     place = lax.axis_index("tm")
     chip, core = place // 2, lax.rem(place, 2)
     chips, rows, order_dim = out.shape
+    total[...] = one[...] + two[...]
 
     @pl.when(chip == 0)
     def _():
         for k in range(chips):
             out[k] = total[pl.ds(pl.multiple_of((2 * k + core) * rows, 8), rows), :]
 
-    def run(mine):
+    @pl.when(chip > 0)
+    def _():
         left = parts(mine[...].reshape(chips * rows, order_dim))
         out[...] = mul(left, parts(total[...])).reshape(out.shape)
 
-    pl.when(chip == 1)(lambda: run(near))
-    pl.when(chip == 3)(lambda: run(far))
-
-
-def right_kernel(near, near_other, across, across_other, far, far_other, left, total, out, whole):
+
+def right_kernel(mine, theirs, left, out, whole):
     place = lax.axis_index("tm")
     chip, core = place // 2, lax.rem(place, 2)
     chips, rows, order_dim = out.shape
-    tall, square = (chips * rows, order_dim), total.shape
 
     @pl.when(chip == 0)
     def _():
         out[...] = left[...]
 
-    def run(mine, theirs):
+    @pl.when(chip > 0)
+    def _():
         fill(whole, core, mine, theirs)
-        right = parts(whole[...].reshape(square))
-        out[...] = mul(parts(left[...].reshape(tall)), right, 1).reshape(out.shape)
-
-    pl.when(chip == 1)(lambda: run(near, near_other))
-    pl.when(chip == 3)(lambda: run(far, far_other))
-
-    @pl.when(chip == 2)
-    def _():
-        fill(whole, core, far, far_other)
-        right = parts(whole[...].reshape(square))
-        value = mul(parts(across[...].reshape(tall)), right)
-        value = mul(parts(mul(parts(value), parts(total[...]))), right, 1)
-        fill(whole, core, across, across_other)
-        right = parts(whole[...].reshape(square))
-        out[...] = mul(parts(value), right, 1).reshape(out.shape)
+        right = parts(whole[...].reshape(order_dim, order_dim))
+        out[...] = mul(parts(left[...].reshape(chips * rows, order_dim)), right, 1).reshape(out.shape)
 
 
 def body(propagators, perturbation):
@@ -157,35 +188,34 @@
     chip = lax.axis_index("tm") // 2
     swap = lambda x: lax.ppermute(x, "tm", [(i, i ^ 1) for i in range(devices)])
     cube = 2 * order_dim**3
+    block_rows = perturbation.shape[1]
     half_shape = (chips, out_rows, order_dim)
     whole_shape = (chips, 2, out_rows, order_dim)
 
     own = propagators[0]
     rows = perturbation[0]
     other = swap(own)
-    blocks = [rows]
-    for shift in range(1, planes):
-        blocks.append(lax.ppermute(rows, "group", [(i, (i + shift) % planes) for i in range(planes)]))
-    (own,) = call(load_kernel, [own.shape], [own])
+    own, part = call(load_kernel, [own.shape, (block_rows, order_dim // 3 * 2)], [own, rows])
+    near = {}
+    for name, sent, way in (("beside", rows, 1), ("skip", part, 2), ("cross", part, 3)):
+        near[name] = lax.ppermute(sent, "group", [(i, i ^ way) for i in range(planes)])
     half, even_t = call(pair_kernel, [half_shape, own.shape], [own, other], [half_shape], 2 * cube)
 
-    mine, theirs = {}, {}
-    for way in (2, 1, 3):
-        pairs = [(i, i ^ (2 * way)) for i in range(devices) if i < i ^ (2 * way)]
-        mine[way] = lax.ppermute(half, "tm", pairs)
-    for way in (2, 1, 3):
-        theirs[way] = swap(mine[way])
-    operands = [mine[1], theirs[1], mine[2], theirs[2]]
-    (chain,) = call(chain_kernel, [own.shape], operands, [whole_shape], 2 * cube)
-    blocks_other = []
-    for shift in range(planes):
-        blocks_other.append(swap(blocks[shift]))
-    operands = blocks + blocks_other + [even_t, chain]
-    kernel = functools.partial(local_kernel, planes)
-    (total,) = call(kernel, [own.shape], operands, [(2,) + own.shape], 12 * cube)
-    (left,) = call(left_kernel, [half_shape], [mine[1], mine[3], total], [], 2 * cube)
-    operands = [x[way] for way in (1, 2, 3) for x in (mine, theirs)] + [left, total]
-    (terms,) = call(right_kernel, [half_shape], operands, [whole_shape], 2 * cube)
+    routes = {"skip": [(1, 3)], "step": [(0, 1), (1, 2), (2, 3)], "far": [(0, 3)], "across": [(0, 2)]}
+    got, other = {}, {}
+    for name, links in routes.items():
+        got[name] = lax.ppermute(half, "tm", [(2 * i + c, 2 * j + c) for i, j in links for c in range(2)])
+    for name in ("skip", "step"):
+        other[name] = swap(got[name])
+    operands = [even_t] + [x[name] for name in ("step", "skip") for x in (got, other)]
+    (carry,) = call(carry_kernel, [own.shape], operands, [whole_shape], 2 * cube)
+    operands = [rows] + [near[name] for name in ("beside", "skip", "cross")] + [carry]
+    (one,) = call(local_kernel, [own.shape], operands, [own.shape], 6 * cube)
+    two = swap(one)
+    (mine,) = call(pick_kernel, [half_shape], [got[name] for name in ("step", "across", "far")])
+    theirs = swap(mine)
+    (left,) = call(left_kernel, [half_shape], [mine, one, two], [own.shape], 2 * cube)
+    (terms,) = call(right_kernel, [half_shape], [mine, theirs, left], [whole_shape], 2 * cube)
     out = lax.dynamic_index_in_dim(terms, chip, 0, False)
     for way in (3, 2, 1):
         block = lax.dynamic_index_in_dim(terms, chip ^ way, 0, False)
@@ -246,8 +276,8 @@
 
     def step(propagators, perturbation):
         order_dim = propagators.shape[1]
-        tiled = order_dim // planes % 8 == 0 and order_dim // (2 * chips) % 8 == 0
-        plan = body if tiled and chips == 4 else plain_body
+        tiled = order_dim // planes % 8 == 0 and order_dim // (2 * chips) % 8 == 0 and order_dim % 384 == 0
+        plan = body if tiled and chips == 4 and planes == 4 else plain_body
         return jax.shard_map(plan, mesh=mesh, in_specs=in_specs, out_specs=out_specs, check_vma=False)(
             propagators, perturbation
         )

time: 49.9 us -> 53.9 us (1.080)
  the two profiles are of different devices: /device:TPU:24 before, /device:TPU:0 now
where the time goes in v4:
time: 53.9 us; the launch traced here: 53.7 us
  waiting for transfers between devices  26 us (48%)
  starting transfers between devices  23.8 us (44%)
  local copies, waits for them, and re-layouts  2.01 us (4%)
  Pallas kernels  1.14 us (2%)
  other arithmetic  0.65 us (1%)
    ppermute x4, starting transfers between devices, body(): lax.ppermute(half, 'tm', [(2 * i + c, 2 * j + c) for i, j in links for c...  13.3 us
    ppermute x4, waiting for transfers between devices, body(): lax.ppermute(half, 'tm', [(2 * i + c, 2 * j + c) for i, j in links for c...  12.9 us
    ppermute x3, waiting for transfers between devices, body(): lax.ppermute(sent, 'group', [(i, i ^ way) for i in range(planes)])  7.85 us
    ppermute x3, starting transfers between devices, body(): lax.ppermute(block, 'tm', [(i, i ^ 2 * way) for i in range(devices)])  4.68 us
    ppermute x3, starting transfers between devices, body(): lax.ppermute(sent, 'group', [(i, i ^ way) for i in range(planes)])  4.39 us
    ppermute x3, waiting for transfers between devices, body(): lax.ppermute(block, 'tm', [(i, i ^ 2 * way) for i in range(devices)])  3.71 us
    unnamed x6, local copies, waits for them, and re-layouts  1.98 us
    ppermute x5, waiting for transfers between devices, body(): swap = lambda x: lax.ppermute(x, 'tm', [(i, i ^ 1) for i in range(devices)])  1.5 us
  transfers between devices with their start and end apart: 15, of which 7 were waited for; matrix products, arithmetic and copies ran while one was open for 0% of the time, Pallas kernels for 0%

profile of v4, /device:TPU:0, one launch (start us, length us, event | category | flops | bytes accessed | tf_op | source)
XLA Modules:
  0.0 53.7 jit_solution(7086904061482229380)
XLA Ops:
  0.0 0.5 collective-permute-start
  0.5 0.0 copy-start
  0.5 1.1 %copy-done = f32[1,384,384]{2,1,0:T(8,128)S(1)} copy-done((f32[1,384,384]{2,1,0:T(8,128)S(1)}, f32[1,384,384]{2,1,0:T(8,128)}, u32[]{:S(2)}) %copy-start) | copy-done | bytes 589848
  1.6 0.0 copy-start.1
  1.6 0.9 %copy-done.1 = f32[1,96,384]{2,1,0:T(8,128)S(1)} copy-done((f32[1,96,384]{2,1,0:T(8,128)S(1)}, f32[1,96,384]{2,1,0:T(8,128)}, u32[]{:S(2)}) %copy-start.1) | copy-done | bytes 147480
  2.5 0.0 collective-permute-done.other
  2.5 0.0 copy-start.2
  2.5 0.7 %shard_map.29 = (f32[4,48,384]{2,1,0:T(8,128)S(1)}, f32[384,384]{1,0:T(8,128)S(1)}) custom-call(f32[384,384]{1,0:T(8,128)S(1)} %get-tuple-element.9.own, f32[384,384]{1,0:T(8,128)S(1)} %collective-permute-done.other), custom_call_target="tpu_custom_call" | custom-call | flops 226492416 | tf_op jit(solution)/shard_map/pallas_call | solution.py:31
  3.2 4.5 %collective-permute-start.1 = (f32[4,48,384]{2,1,0:T(8,128)S(1)}, f32[4,48,384]{2,1,0:T(8,128)S(1)}, u32[]{:S(2)}, u32[]{:S(2)}) collective-permute-start(f32[4,48,384]{2,1,0:T(8,128)S(1)} %get-tuple-element.10), channel_id=1, source_target_pairs={{0,8},{4,12},{8,16},{12,20},{16,24},{20,28},{1,9},{5,13},{9,17},{1... | collective-permute-start | bytes 884744 | tf_op jit(solution)/shard_map/ppermute | solution.py:207
  7.8 0.7 %collective-permute-start.9 = (f32[4,48,384]{2,1,0:T(8,128)S(1)}, f32[4,48,384]{2,1,0:T(8,128)S(1)}, u32[]{:S(2)}, u32[]{:S(2)}) collective-permute-start(f32[4,48,384]{2,1,0:T(8,128)S(1)} %get-tuple-element.10), channel_id=1, source_target_pairs={{8,24},{12,28},{9,25},{13,29},{10,26},{14,30},{11,27},{15,31}} | collective-permute-start | bytes 884744 | tf_op jit(solution)/shard_map/ppermute | solution.py:207
  8.5 6.1 %collective-permute-done.1.first.step = f32[4,48,384]{2,1,0:T(8,128)S(1)} collective-permute-done((f32[4,48,384]{2,1,0:T(8,128)S(1)}, f32[4,48,384]{2,1,0:T(8,128)S(1)}, u32[]{:S(2)}, u32[]{:S(2)}) %collective-permute-start.1) | collective-permute-done | bytes 294944 | tf_op jit(solution)/shard_map/ppermute | solution.py:207
  14.5 0.0 collective-permute-start.8
  14.5 0.0 collective-permute-done.9.skip
  14.5 0.5 collective-permute-start.10
  15.0 0.0 copy-done.2
  15.0 1.6 %collective-permute-start.5 = (f32[96,384]{1,0:T(8,128)S(1)}, f32[96,384]{1,0:T(8,128)S(1)}, u32[]{:S(2)}, u32[]{:S(2)}) collective-permute-start(f32[96,384]{1,0:T(8,128)S(1)} %bitcast.17), channel_id=1, source_target_pairs={{0,1},{1,0},{2,3},{3,2},{4,5},{5,4},{6,7},{7,6},{8,9},{9,8},{10,11... | collective-permute-start | bytes 442376 | tf_op jit(solution)/shard_map/ppermute | solution.py:201
  16.6 2.6 %collective-permute-start.6 = (f32[96,256]{1,0:T(8,128)S(1)}, f32[96,256]{1,0:T(8,128)S(1)}, u32[]{:S(2)}, u32[]{:S(2)}) collective-permute-start(f32[96,256]{1,0:T(8,128)S(1)} %get-tuple-element.11), channel_id=1, source_target_pairs={{0,2},{1,3},{2,0},{3,1},{4,6},{5,7},{6,4},{7,5},{8,10},{9,11},{10,... | collective-permute-start | bytes 294920 | tf_op jit(solution)/shard_map/ppermute | solution.py:201
  19.2 0.2 collective-permute-start.7
  19.4 0.0 collective-permute-done.8.step_other
  19.4 0.0 collective-permute-done.10.skip_other
  19.4 7.8 %collective-permute-done.6.skip = f32[96,256]{1,0:T(8,128)S(1)} collective-permute-done((f32[96,256]{1,0:T(8,128)S(1)}, f32[96,256]{1,0:T(8,128)S(1)}, u32[]{:S(2)}, u32[]{:S(2)}) %collective-permute-start.6) | collective-permute-done | bytes 98336 | tf_op jit(solution)/shard_map/ppermute | solution.py:201
  27.3 0.0 collective-permute-done.7.cross
  27.3 0.0 collective-permute-done.5.beside
  27.3 0.3 shard_map.32.one
  27.6 0.3 collective-permute-start.11
  28.0 6.3 %collective-permute-start.2 = (f32[4,48,384]{2,1,0:T(8,128)S(1)}, f32[4,48,384]{2,1,0:T(8,128)S(1)}, u32[]{:S(2)}, u32[]{:S(2)}) collective-permute-start(f32[4,48,384]{2,1,0:T(8,128)S(1)} %get-tuple-element.10), channel_id=1, source_target_pairs={{0,16},{4,20},{1,17},{5,21},{2,18},{6,22},{3,19},{7,23}} | collective-permute-start | bytes 884744 | tf_op jit(solution)/shard_map/ppermute | solution.py:207
  34.2 1.8 %collective-permute-start.3 = (f32[4,48,384]{2,1,0:T(8,128)S(1)}, f32[4,48,384]{2,1,0:T(8,128)S(1)}, u32[]{:S(2)}, u32[]{:S(2)}) collective-permute-start(f32[4,48,384]{2,1,0:T(8,128)S(1)} %get-tuple-element.10), channel_id=1, source_target_pairs={{0,24},{4,28},{1,25},{5,29},{2,26},{6,30},{3,27},{7,31}} | collective-permute-start | bytes 884744 | tf_op jit(solution)/shard_map/ppermute | solution.py:207
  36.1 5.0 %collective-permute-done.2.second = f32[4,48,384]{2,1,0:T(8,128)S(1)} collective-permute-done((f32[4,48,384]{2,1,0:T(8,128)S(1)}, f32[4,48,384]{2,1,0:T(8,128)S(1)}, u32[]{:S(2)}, u32[]{:S(2)}) %collective-permute-start.2) | collective-permute-done | bytes 294944 | tf_op jit(solution)/shard_map/ppermute | solution.py:207
  41.1 1.9 %collective-permute-done.3.third = f32[4,48,384]{2,1,0:T(8,128)S(1)} collective-permute-done((f32[4,48,384]{2,1,0:T(8,128)S(1)}, f32[4,48,384]{2,1,0:T(8,128)S(1)}, u32[]{:S(2)}, u32[]{:S(2)}) %collective-permute-start.3) | collective-permute-done | bytes 294944 | tf_op jit(solution)/shard_map/ppermute | solution.py:207
  43.0 0.0 collective-permute-start.4
  43.0 0.0 collective-permute-done.11.two
  43.0 0.1 shard_map.33.left
  43.1 1.5 %collective-permute-done.4.theirs = f32[4,48,384]{2,1,0:T(8,128)S(1)} collective-permute-done((f32[4,48,384]{2,1,0:T(8,128)S(1)}, f32[4,48,384]{2,1,0:T(8,128)S(1)}, u32[]{:S(2)}, u32[]{:S(2)}) %collective-permute-start.4) | collective-permute-done | bytes 294944 | tf_op jit(solution)/shard_map/ppermute | solution.py:189
  44.6 4.0 %collective-permute-start.12 = (f32[48,384]{1,0:T(8,128)S(1)}, f32[48,384]{1,0:T(8,128)S(1)}, u32[]{:S(2)}, u32[]{:S(2)}) collective-permute-start(f32[48,384]{1,0:T(8,128)S(1)} %get-tuple-element.13), channel_id=1, source_target_pairs={{0,24},{4,28},{8,16},{12,20},{16,8},{20,12},{24,0},{28,4},{1,25},{... | collective-permute-start | bytes 221192 | tf_op jit(solution)/shard_map/ppermute | solution.py:222
  48.7 0.0 collective-permute-start.13
  48.7 0.6 %collective-permute-start.14 = (f32[48,384]{1,0:T(8,128)S(1)}, f32[48,384]{1,0:T(8,128)S(1)}, u32[]{:S(2)}, u32[]{:S(2)}) collective-permute-start(f32[48,384]{1,0:T(8,128)S(1)} %get-tuple-element.14), channel_id=1, source_target_pairs={{0,8},{4,12},{8,0},{12,4},{16,24},{20,28},{24,16},{28,20},{1,9},{5... | collective-permute-start | bytes 221192 | tf_op jit(solution)/shard_map/ppermute | solution.py:222
  49.3 2.0 %collective-permute-done.12 = f32[48,384]{1,0:T(8,128)S(1)} collective-permute-done((f32[48,384]{1,0:T(8,128)S(1)}, f32[48,384]{1,0:T(8,128)S(1)}, u32[]{:S(2)}, u32[]{:S(2)}) %collective-permute-start.12) | collective-permute-done | bytes 73760 | tf_op jit(solution)/shard_map/ppermute | solution.py:222
  51.3 1.7 %collective-permute-done.13 = f32[48,384]{1,0:T(8,128)S(1)} collective-permute-done((f32[48,384]{1,0:T(8,128)S(1)}, f32[48,384]{1,0:T(8,128)S(1)}, u32[]{:S(2)}, u32[]{:S(2)}) %collective-permute-start.13) | collective-permute-done | bytes 73760 | tf_op jit(solution)/shard_map/ppermute | solution.py:222
  53.0 0.0 collective-permute-done.14
  53.0 0.7 %fusion.1 = f32[48,384]{1,0:T(8,128)} fusion(f32[48,384]{1,0:T(8,128)S(1)} %collective-permute-done.14, f32[48,384]{1,0:T(8,128)S(1)} %collective-permute-done.13, f32[48,384]{1,0:T(8,128)S(1)} %collective-permute-done.12, f32[4,48,384]{2,1,0:T(8,128)S(1)} %shard_map.34, s32[]{:T(128)S(6)} %select_n.19), kind=kLoop, calls=%fused_computation.2 | loop fusion | flops 55296 | bytes 368644 | tf_op jit(solution)/shard_map/add | solution.py:222
  (5 shorter events, 0.1 us)
Async XLA Ops:
  0.0 2.5 %collective-permute-start = (f32[384,384]{1,0:T(8,128)}, f32[384,384]{1,0:T(8,128)S(1)}, u32[]{:S(2)}, u32[]{:S(2)}) collective-permute-start(f32[384,384]{1,0:T(8,128)} %bitcast.14), channel_id=1, source_target_pairs={{0,4},{4,0},{8,12},{12,8},{16,20},{20,16},{24,28},{28,24},{1,5},{5... | collective-permute-start | bytes 1769480 | tf_op jit(solution)/shard_map/ppermute | solution.py:189
  0.5 1.1 %copy-start = (f32[1,384,384]{2,1,0:T(8,128)S(1)}, f32[1,384,384]{2,1,0:T(8,128)}, u32[]{:S(2)}) copy-start(f32[1,384,384]{2,1,0:T(8,128)} %param.2) | copy-start | bytes 1769476
  1.6 0.9 %copy-start.1 = (f32[1,96,384]{2,1,0:T(8,128)S(1)}, f32[1,96,384]{2,1,0:T(8,128)}, u32[]{:S(2)}) copy-start(f32[1,96,384]{2,1,0:T(8,128)} %param.3) | copy-start | bytes 442372
  2.5 12.5 %copy-start.2 = (f32[1,96,384]{2,1,0:T(8,128)S(1)}, f32[1,96,384]{2,1,0:T(8,128)}, u32[]{:S(2)}) copy-start(f32[1,96,384]{2,1,0:T(8,128)} %param.3) | copy-start | bytes 442372
  3.2 11.3 %collective-permute-start.1 = (f32[4,48,384]{2,1,0:T(8,128)S(1)}, f32[4,48,384]{2,1,0:T(8,128)S(1)}, u32[]{:S(2)}, u32[]{:S(2)}) collective-permute-start(f32[4,48,384]{2,1,0:T(8,128)S(1)} %get-tuple-element.10), channel_id=1, source_target_pairs={{0,8},{4,12},{8,16},{12,20},{16,24},{20,28},{1,9},{5,13},{9,17},{1... | collective-permute-start | bytes 884744 | tf_op jit(solution)/shard_map/ppermute | solution.py:207
  7.8 6.7 %collective-permute-start.9 = (f32[4,48,384]{2,1,0:T(8,128)S(1)}, f32[4,48,384]{2,1,0:T(8,128)S(1)}, u32[]{:S(2)}, u32[]{:S(2)}) collective-permute-start(f32[4,48,384]{2,1,0:T(8,128)S(1)} %get-tuple-element.10), channel_id=1, source_target_pairs={{8,24},{12,28},{9,25},{13,29},{10,26},{14,30},{11,27},{15,31}} | collective-permute-start | bytes 884744 | tf_op jit(solution)/shard_map/ppermute | solution.py:207
  14.5 4.9 %collective-permute-start.8 = (f32[4,48,384]{2,1,0:T(8,128)S(1)}, f32[4,48,384]{2,1,0:T(8,128)S(1)}, u32[]{:S(2)}, u32[]{:S(2)}) collective-permute-start(f32[4,48,384]{2,1,0:T(8,128)S(1)} %collective-permute-done.1.first.step), channel_id=1, source_target_pairs={{0,4},{4,0},{8,12},{12,8},{16,20},{20,16},{24,28},{28,24},{1,5},{5... | collective-permute-start | bytes 884744 | tf_op jit(solution)/shard_map/ppermute | solution.py:189
  14.5 4.9 %collective-permute-start.10 = (f32[4,48,384]{2,1,0:T(8,128)S(1)}, f32[4,48,384]{2,1,0:T(8,128)S(1)}, u32[]{:S(2)}, u32[]{:S(2)}) collective-permute-start(f32[4,48,384]{2,1,0:T(8,128)S(1)} %collective-permute-done.9.skip), channel_id=1, source_target_pairs={{0,4},{4,0},{8,12},{12,8},{16,20},{20,16},{24,28},{28,24},{1,5},{5... | collective-permute-start | bytes 884744 | tf_op jit(solution)/shard_map/ppermute | solution.py:189
  15.0 12.2 %collective-permute-start.5 = (f32[96,384]{1,0:T(8,128)S(1)}, f32[96,384]{1,0:T(8,128)S(1)}, u32[]{:S(2)}, u32[]{:S(2)}) collective-permute-start(f32[96,384]{1,0:T(8,128)S(1)} %bitcast.17), channel_id=1, source_target_pairs={{0,1},{1,0},{2,3},{3,2},{4,5},{5,4},{6,7},{7,6},{8,9},{9,8},{10,11... | collective-permute-start | bytes 442376 | tf_op jit(solution)/shard_map/ppermute | solution.py:201
  16.6 10.7 %collective-permute-start.6 = (f32[96,256]{1,0:T(8,128)S(1)}, f32[96,256]{1,0:T(8,128)S(1)}, u32[]{:S(2)}, u32[]{:S(2)}) collective-permute-start(f32[96,256]{1,0:T(8,128)S(1)} %get-tuple-element.11), channel_id=1, source_target_pairs={{0,2},{1,3},{2,0},{3,1},{4,6},{5,7},{6,4},{7,5},{8,10},{9,11},{10,... | collective-permute-start | bytes 294920 | tf_op jit(solution)/shard_map/ppermute | solution.py:201
  19.2 8.1 %collective-permute-start.7 = (f32[96,256]{1,0:T(8,128)S(1)}, f32[96,256]{1,0:T(8,128)S(1)}, u32[]{:S(2)}, u32[]{:S(2)}) collective-permute-start(f32[96,256]{1,0:T(8,128)S(1)} %get-tuple-element.11), channel_id=1, source_target_pairs={{0,3},{1,2},{2,1},{3,0},{4,7},{5,6},{6,5},{7,4},{8,11},{9,10},{10,... | collective-permute-start | bytes 294920 | tf_op jit(solution)/shard_map/ppermute | solution.py:201
  27.6 15.4 %collective-permute-start.11 = (f32[384,384]{1,0:T(8,128)S(1)}, f32[384,384]{1,0:T(8,128)S(1)}, u32[]{:S(2)}, u32[]{:S(2)}) collective-permute-start(f32[384,384]{1,0:T(8,128)S(1)} %shard_map.32.one), channel_id=1, source_target_pairs={{0,4},{4,0},{8,12},{12,8},{16,20},{20,16},{24,28},{28,24},{1,5},{5... | collective-permute-start | bytes 1769480 | tf_op jit(solution)/shard_map/ppermute | solution.py:189
  28.0 13.2 %collective-permute-start.2 = (f32[4,48,384]{2,1,0:T(8,128)S(1)}, f32[4,48,384]{2,1,0:T(8,128)S(1)}, u32[]{:S(2)}, u32[]{:S(2)}) collective-permute-start(f32[4,48,384]{2,1,0:T(8,128)S(1)} %get-tuple-element.10), channel_id=1, source_target_pairs={{0,16},{4,20},{1,17},{5,21},{2,18},{6,22},{3,19},{7,23}} | collective-permute-start | bytes 884744 | tf_op jit(solution)/shard_map/ppermute | solution.py:207
  34.2 8.7 %collective-permute-start.3 = (f32[4,48,384]{2,1,0:T(8,128)S(1)}, f32[4,48,384]{2,1,0:T(8,128)S(1)}, u32[]{:S(2)}, u32[]{:S(2)}) collective-permute-start(f32[4,48,384]{2,1,0:T(8,128)S(1)} %get-tuple-element.10), channel_id=1, source_target_pairs={{0,24},{4,28},{1,25},{5,29},{2,26},{6,30},{3,27},{7,31}} | collective-permute-start | bytes 884744 | tf_op jit(solution)/shard_map/ppermute | solution.py:207
  43.0 1.6 %collective-permute-start.4 = (f32[4,48,384]{2,1,0:T(8,128)S(1)}, f32[4,48,384]{2,1,0:T(8,128)S(1)}, u32[]{:S(2)}, u32[]{:S(2)}) collective-permute-start(f32[4,48,384]{2,1,0:T(8,128)S(1)} %shard_map.30.mine), channel_id=1, source_target_pairs={{0,4},{4,0},{8,12},{12,8},{16,20},{20,16},{24,28},{28,24},{1,5},{5... | collective-permute-start | bytes 884744 | tf_op jit(solution)/shard_map/ppermute | solution.py:189
  44.6 6.7 %collective-permute-start.12 = (f32[48,384]{1,0:T(8,128)S(1)}, f32[48,384]{1,0:T(8,128)S(1)}, u32[]{:S(2)}, u32[]{:S(2)}) collective-permute-start(f32[48,384]{1,0:T(8,128)S(1)} %get-tuple-element.13), channel_id=1, source_target_pairs={{0,24},{4,28},{8,16},{12,20},{16,8},{20,12},{24,0},{28,4},{1,25},{... | collective-permute-start | bytes 221192 | tf_op jit(solution)/shard_map/ppermute | solution.py:222
  48.7 4.4 %collective-permute-start.13 = (f32[48,384]{1,0:T(8,128)S(1)}, f32[48,384]{1,0:T(8,128)S(1)}, u32[]{:S(2)}, u32[]{:S(2)}) collective-permute-start(f32[48,384]{1,0:T(8,128)S(1)} %get-tuple-element.15), channel_id=1, source_target_pairs={{0,16},{4,20},{8,24},{12,28},{16,0},{20,4},{24,8},{28,12},{1,17},{... | collective-permute-start | bytes 221192 | tf_op jit(solution)/shard_map/ppermute | solution.py:222
  48.7 4.4 %collective-permute-start.14 = (f32[48,384]{1,0:T(8,128)S(1)}, f32[48,384]{1,0:T(8,128)S(1)}, u32[]{:S(2)}, u32[]{:S(2)}) collective-permute-start(f32[48,384]{1,0:T(8,128)S(1)} %get-tuple-element.14), channel_id=1, source_target_pairs={{0,8},{4,12},{8,0},{12,4},{16,24},{20,28},{24,16},{28,20},{1,9},{5... | collective-permute-start | bytes 221192 | tf_op jit(solution)/shard_map/ppermute | solution.py:222

commit v5 on v4

--- a/solution.py
+++ b/solution.py
@@ -39,10 +39,11 @@
     )(*operands)
 
 
-def load_kernel(own, rows, copy, part):
+def load_kernel(own, rows, copy, rows_copy, part):
     plane = lax.axis_index("group")
     lanes = part.shape[1]
     copy[...] = own[...]
+    rows_copy[...] = rows[...]
 
     @pl.when(plane < 2)
     def _():
@@ -54,8 +55,10 @@
 
 
 def pair_kernel(own, other, half, even_t, work):
-    core = lax.rem(lax.axis_index("tm"), 2)
+    place = lax.axis_index("tm")
+    chip, core = place // 2, lax.rem(place, 2)
     chips, rows, order_dim = half.shape
+    used = chip < chips - 1
 
     def run(even, odd):
         even_t[...] = even[...].T
@@ -65,8 +68,8 @@
         left = parts(work[...].reshape(chips * rows, order_dim))
         half[...] = mul(left, parts(odd[...]), 1).reshape(half.shape)
 
-    pl.when(core == 0)(lambda: run(own, other))
-    pl.when(core == 1)(lambda: run(other, own))
+    pl.when(used & (core == 0))(lambda: run(own, other))
+    pl.when(used & (core == 1))(lambda: run(other, own))
 
 
 def fill(whole, core, mine, theirs):
@@ -74,7 +77,7 @@
     whole[:, 1 - core] = theirs[...]
 
 
-def carry_kernel(even_t, step, step_other, skip, skip_other, out, whole):
+def carry_kernel(even_t, even, step, step_other, skip, skip_other, out, whole):
     place = lax.axis_index("tm")
     chip, core = place // 2, lax.rem(place, 2)
     shape = out.shape
@@ -93,9 +96,13 @@
         fill(whole, core, skip, skip_other)
         out[...] = mul(parts(whole[...].reshape(shape)), parts(out[...]))
 
-    @pl.when((chip >= 2) & (core == 1))
+    @pl.when((chip == 2) & (core == 1))
     def _():
         out[...] = mul(parts(out[...]), parts(even_t[...]))
+
+    @pl.when((chip == 3) & (core == 1))
+    def _():
+        out[...] = mul(parts(out[...]), parts(even[...]), 1)
 
 
 def local_kernel(rows, beside, skip, cross, carry, out, full):
@@ -195,19 +202,20 @@
     own = propagators[0]
     rows = perturbation[0]
     other = swap(own)
-    own, part = call(load_kernel, [own.shape, (block_rows, order_dim // 3 * 2)], [own, rows])
+    shapes = [own.shape, rows.shape, (block_rows, order_dim // 3 * 2)]
+    own, rows, part = call(load_kernel, shapes, [own, rows])
     near = {}
     for name, sent, way in (("beside", rows, 1), ("skip", part, 2), ("cross", part, 3)):
         near[name] = lax.ppermute(sent, "group", [(i, i ^ way) for i in range(planes)])
     half, even_t = call(pair_kernel, [half_shape, own.shape], [own, other], [half_shape], 2 * cube)
 
     routes = {"skip": [(1, 3)], "step": [(0, 1), (1, 2), (2, 3)], "far": [(0, 3)], "across": [(0, 2)]}
-    got, other = {}, {}
+    got, paired = {}, {}
     for name, links in routes.items():
         got[name] = lax.ppermute(half, "tm", [(2 * i + c, 2 * j + c) for i, j in links for c in range(2)])
     for name in ("skip", "step"):
-        other[name] = swap(got[name])
-    operands = [even_t] + [x[name] for name in ("step", "skip") for x in (got, other)]
+        paired[name] = swap(got[name])
+    operands = [even_t, other] + [x[name] for name in ("step", "skip") for x in (got, paired)]
     (carry,) = call(carry_kernel, [own.shape], operands, [whole_shape], 2 * cube)
     operands = [rows] + [near[name] for name in ("beside", "skip", "cross")] + [carry]
     (one,) = call(local_kernel, [own.shape], operands, [own.shape], 6 * cube)

time: 53.9 us -> 53.9 us (level)
    unnamed x6 -> x4, local copies, waits for them, and re-layouts: 1.98 us -> 1.97 us
where the time goes in v5:
time: 53.9 us; the launch traced here: 53.6 us
  waiting for transfers between devices  26.1 us (48%)
  starting transfers between devices  23.7 us (44%)
  local copies, waits for them, and re-layouts  2 us (4%)
  Pallas kernels  1.15 us (2%)
  other arithmetic  0.65 us (1%)
    ppermute x4, starting transfers between devices, body(): lax.ppermute(half, 'tm', [(2 * i + c, 2 * j + c) for i, j in links for c...  13.4 us
    ppermute x4, waiting for transfers between devices, body(): lax.ppermute(half, 'tm', [(2 * i + c, 2 * j + c) for i, j in links for c...  12.9 us
    ppermute x3, waiting for transfers between devices, body(): lax.ppermute(sent, 'group', [(i, i ^ way) for i in range(planes)])  7.92 us
    ppermute x3, starting transfers between devices, body(): lax.ppermute(block, 'tm', [(i, i ^ 2 * way) for i in range(devices)])  4.68 us
    ppermute x3, starting transfers between devices, body(): lax.ppermute(sent, 'group', [(i, i ^ way) for i in range(planes)])  4.39 us
    ppermute x3, waiting for transfers between devices, body(): lax.ppermute(block, 'tm', [(i, i ^ 2 * way) for i in range(devices)])  3.71 us
    unnamed x4, local copies, waits for them, and re-layouts  1.97 us
    ppermute x5, waiting for transfers between devices, body(): swap = lambda x: lax.ppermute(x, 'tm', [(i, i ^ 1) for i in range(devices)])  1.5 us
  transfers between devices with their start and end apart: 15, of which 7 were waited for; matrix products, arithmetic and copies ran while one was open for 0% of the time, Pallas kernels for 0%

profile of v5, /device:TPU:0, one launch (start us, length us, event | category | flops | bytes accessed | tf_op | source)
XLA Modules:
  0.0 53.6 jit_solution(12813636726718818337)
XLA Ops:
  0.0 0.5 collective-permute-start
  0.5 0.0 copy-start
  0.5 1.1 %copy-done = f32[1,384,384]{2,1,0:T(8,128)S(1)} copy-done((f32[1,384,384]{2,1,0:T(8,128)S(1)}, f32[1,384,384]{2,1,0:T(8,128)}, u32[]{:S(2)}) %copy-start) | copy-done | bytes 589848
  1.6 0.0 copy-start.1
  1.6 0.9 %copy-done.1 = f32[1,96,384]{2,1,0:T(8,128)S(1)} copy-done((f32[1,96,384]{2,1,0:T(8,128)S(1)}, f32[1,96,384]{2,1,0:T(8,128)}, u32[]{:S(2)}) %copy-start.1) | copy-done | bytes 147480
  2.5 0.1 shard_map.28
  2.5 0.0 collective-permute-done.other.even
  2.5 0.7 %shard_map.29 = (f32[4,48,384]{2,1,0:T(8,128)S(1)}, f32[384,384]{1,0:T(8,128)S(1)}) custom-call(f32[384,384]{1,0:T(8,128)S(1)} %get-tuple-element.10.own, f32[384,384]{1,0:T(8,128)S(1)} %collective-permute-done.other.even), custom_call_target="tpu_custom_call" | custom-call | flops 226492416 | tf_op jit(solution)/shard_map/pallas_call | solution.py:31
  3.2 4.5 %collective-permute-start.1 = (f32[4,48,384]{2,1,0:T(8,128)S(1)}, f32[4,48,384]{2,1,0:T(8,128)S(1)}, u32[]{:S(2)}, u32[]{:S(2)}) collective-permute-start(f32[4,48,384]{2,1,0:T(8,128)S(1)} %get-tuple-element.11), channel_id=1, source_target_pairs={{0,8},{4,12},{8,16},{12,20},{16,24},{20,28},{1,9},{5,13},{9,17},{1... | collective-permute-start | bytes 884744 | tf_op jit(solution)/shard_map/ppermute | solution.py:215
  7.8 0.7 %collective-permute-start.9 = (f32[4,48,384]{2,1,0:T(8,128)S(1)}, f32[4,48,384]{2,1,0:T(8,128)S(1)}, u32[]{:S(2)}, u32[]{:S(2)}) collective-permute-start(f32[4,48,384]{2,1,0:T(8,128)S(1)} %get-tuple-element.11), channel_id=1, source_target_pairs={{8,24},{12,28},{9,25},{13,29},{10,26},{14,30},{11,27},{15,31}} | collective-permute-start | bytes 884744 | tf_op jit(solution)/shard_map/ppermute | solution.py:215
  8.5 6.1 %collective-permute-done.1.first.step = f32[4,48,384]{2,1,0:T(8,128)S(1)} collective-permute-done((f32[4,48,384]{2,1,0:T(8,128)S(1)}, f32[4,48,384]{2,1,0:T(8,128)S(1)}, u32[]{:S(2)}, u32[]{:S(2)}) %collective-permute-start.1) | collective-permute-done | bytes 294944 | tf_op jit(solution)/shard_map/ppermute | solution.py:215
  14.5 0.0 collective-permute-start.8
  14.5 0.0 collective-permute-done.9.skip
  14.5 0.5 collective-permute-start.10
  15.0 1.6 %collective-permute-start.5 = (f32[96,384]{1,0:T(8,128)S(1)}, f32[96,384]{1,0:T(8,128)S(1)}, u32[]{:S(2)}, u32[]{:S(2)}) collective-permute-start(f32[96,384]{1,0:T(8,128)S(1)} %get-tuple-element.12.rows), channel_id=1, source_target_pairs={{0,1},{1,0},{2,3},{3,2},{4,5},{5,4},{6,7},{7,6},{8,9},{9,8},{10,11... | collective-permute-start | bytes 442376 | tf_op jit(solution)/shard_map/ppermute | solution.py:209
  16.6 2.6 %collective-permute-start.6 = (f32[96,256]{1,0:T(8,128)S(1)}, f32[96,256]{1,0:T(8,128)S(1)}, u32[]{:S(2)}, u32[]{:S(2)}) collective-permute-start(f32[96,256]{1,0:T(8,128)S(1)} %get-tuple-element.13), channel_id=1, source_target_pairs={{0,2},{1,3},{2,0},{3,1},{4,6},{5,7},{6,4},{7,5},{8,10},{9,11},{10,... | collective-permute-start | bytes 294920 | tf_op jit(solution)/shard_map/ppermute | solution.py:209
  19.2 0.2 collective-permute-start.7
  19.4 0.0 collective-permute-done.8.step_other
  19.4 0.0 collective-permute-done.10.skip_other
  19.4 7.9 %collective-permute-done.6.skip = f32[96,256]{1,0:T(8,128)S(1)} collective-permute-done((f32[96,256]{1,0:T(8,128)S(1)}, f32[96,256]{1,0:T(8,128)S(1)}, u32[]{:S(2)}, u32[]{:S(2)}) %collective-permute-start.6) | collective-permute-done | bytes 98336 | tf_op jit(solution)/shard_map/ppermute | solution.py:209
  27.4 0.0 collective-permute-done.7.cross
  27.4 0.0 collective-permute-done.5.beside
  27.4 0.3 shard_map.32.one
  27.7 0.1 collective-permute-start.11
  27.8 6.5 %collective-permute-start.2 = (f32[4,48,384]{2,1,0:T(8,128)S(1)}, f32[4,48,384]{2,1,0:T(8,128)S(1)}, u32[]{:S(2)}, u32[]{:S(2)}) collective-permute-start(f32[4,48,384]{2,1,0:T(8,128)S(1)} %get-tuple-element.11), channel_id=1, source_target_pairs={{0,16},{4,20},{1,17},{5,21},{2,18},{6,22},{3,19},{7,23}} | collective-permute-start | bytes 884744 | tf_op jit(solution)/shard_map/ppermute | solution.py:215
  34.3 1.8 %collective-permute-start.3 = (f32[4,48,384]{2,1,0:T(8,128)S(1)}, f32[4,48,384]{2,1,0:T(8,128)S(1)}, u32[]{:S(2)}, u32[]{:S(2)}) collective-permute-start(f32[4,48,384]{2,1,0:T(8,128)S(1)} %get-tuple-element.11), channel_id=1, source_target_pairs={{0,24},{4,28},{1,25},{5,29},{2,26},{6,30},{3,27},{7,31}} | collective-permute-start | bytes 884744 | tf_op jit(solution)/shard_map/ppermute | solution.py:215
  36.1 5.1 %collective-permute-done.2.second = f32[4,48,384]{2,1,0:T(8,128)S(1)} collective-permute-done((f32[4,48,384]{2,1,0:T(8,128)S(1)}, f32[4,48,384]{2,1,0:T(8,128)S(1)}, u32[]{:S(2)}, u32[]{:S(2)}) %collective-permute-start.2) | collective-permute-done | bytes 294944 | tf_op jit(solution)/shard_map/ppermute | solution.py:215
  41.2 1.8 %collective-permute-done.3.third = f32[4,48,384]{2,1,0:T(8,128)S(1)} collective-permute-done((f32[4,48,384]{2,1,0:T(8,128)S(1)}, f32[4,48,384]{2,1,0:T(8,128)S(1)}, u32[]{:S(2)}, u32[]{:S(2)}) %collective-permute-start.3) | collective-permute-done | bytes 294944 | tf_op jit(solution)/shard_map/ppermute | solution.py:215
  42.9 0.0 collective-permute-start.4
  43.0 0.0 collective-permute-done.11.two
  43.0 0.1 shard_map.33.left
  43.0 1.5 %collective-permute-done.4.theirs = f32[4,48,384]{2,1,0:T(8,128)S(1)} collective-permute-done((f32[4,48,384]{2,1,0:T(8,128)S(1)}, f32[4,48,384]{2,1,0:T(8,128)S(1)}, u32[]{:S(2)}, u32[]{:S(2)}) %collective-permute-start.4) | collective-permute-done | bytes 294944 | tf_op jit(solution)/shard_map/ppermute | solution.py:196
  44.6 4.0 %collective-permute-start.12 = (f32[48,384]{1,0:T(8,128)S(1)}, f32[48,384]{1,0:T(8,128)S(1)}, u32[]{:S(2)}, u32[]{:S(2)}) collective-permute-start(f32[48,384]{1,0:T(8,128)S(1)} %get-tuple-element.15), channel_id=1, source_target_pairs={{0,24},{4,28},{8,16},{12,20},{16,8},{20,12},{24,0},{28,4},{1,25},{... | collective-permute-start | bytes 221192 | tf_op jit(solution)/shard_map/ppermute | solution.py:230
  48.6 0.0 collective-permute-start.13
  48.6 0.6 %collective-permute-start.14 = (f32[48,384]{1,0:T(8,128)S(1)}, f32[48,384]{1,0:T(8,128)S(1)}, u32[]{:S(2)}, u32[]{:S(2)}) collective-permute-start(f32[48,384]{1,0:T(8,128)S(1)} %get-tuple-element.16), channel_id=1, source_target_pairs={{0,8},{4,12},{8,0},{12,4},{16,24},{20,28},{24,16},{28,20},{1,9},{5... | collective-permute-start | bytes 221192 | tf_op jit(solution)/shard_map/ppermute | solution.py:230
  49.3 2.0 %collective-permute-done.12 = f32[48,384]{1,0:T(8,128)S(1)} collective-permute-done((f32[48,384]{1,0:T(8,128)S(1)}, f32[48,384]{1,0:T(8,128)S(1)}, u32[]{:S(2)}, u32[]{:S(2)}) %collective-permute-start.12) | collective-permute-done | bytes 73760 | tf_op jit(solution)/shard_map/ppermute | solution.py:230
  51.3 1.7 %collective-permute-done.13 = f32[48,384]{1,0:T(8,128)S(1)} collective-permute-done((f32[48,384]{1,0:T(8,128)S(1)}, f32[48,384]{1,0:T(8,128)S(1)}, u32[]{:S(2)}, u32[]{:S(2)}) %collective-permute-start.13) | collective-permute-done | bytes 73760 | tf_op jit(solution)/shard_map/ppermute | solution.py:230
  53.0 0.0 collective-permute-done.14
  53.0 0.7 %fusion.1 = f32[48,384]{1,0:T(8,128)} fusion(f32[48,384]{1,0:T(8,128)S(1)} %collective-permute-done.14, f32[48,384]{1,0:T(8,128)S(1)} %collective-permute-done.13, f32[48,384]{1,0:T(8,128)S(1)} %collective-permute-done.12, f32[4,48,384]{2,1,0:T(8,128)S(1)} %shard_map.34, s32[]{:T(128)S(6)} %select_n.19), kind=kLoop, calls=%fused_computation.2 | loop fusion | flops 55296 | bytes 368644 | tf_op jit(solution)/shard_map/add | solution.py:230
  (4 shorter events, 0.0 us)
Async XLA Ops:
  0.0 2.5 %collective-permute-start = (f32[384,384]{1,0:T(8,128)}, f32[384,384]{1,0:T(8,128)S(1)}, u32[]{:S(2)}, u32[]{:S(2)}) collective-permute-start(f32[384,384]{1,0:T(8,128)} %bitcast.14), channel_id=1, source_target_pairs={{0,4},{4,0},{8,12},{12,8},{16,20},{20,16},{24,28},{28,24},{1,5},{5... | collective-permute-start | bytes 1769480 | tf_op jit(solution)/shard_map/ppermute | solution.py:196
  0.5 1.1 %copy-start = (f32[1,384,384]{2,1,0:T(8,128)S(1)}, f32[1,384,384]{2,1,0:T(8,128)}, u32[]{:S(2)}) copy-start(f32[1,384,384]{2,1,0:T(8,128)} %param.2) | copy-start | bytes 1769476
  1.6 0.9 %copy-start.1 = (f32[1,96,384]{2,1,0:T(8,128)S(1)}, f32[1,96,384]{2,1,0:T(8,128)}, u32[]{:S(2)}) copy-start(f32[1,96,384]{2,1,0:T(8,128)} %param.3) | copy-start | bytes 442372
  3.2 11.3 %collective-permute-start.1 = (f32[4,48,384]{2,1,0:T(8,128)S(1)}, f32[4,48,384]{2,1,0:T(8,128)S(1)}, u32[]{:S(2)}, u32[]{:S(2)}) collective-permute-start(f32[4,48,384]{2,1,0:T(8,128)S(1)} %get-tuple-element.11), channel_id=1, source_target_pairs={{0,8},{4,12},{8,16},{12,20},{16,24},{20,28},{1,9},{5,13},{9,17},{1... | collective-permute-start | bytes 884744 | tf_op jit(solution)/shard_map/ppermute | solution.py:215
  7.8 6.8 %collective-permute-start.9 = (f32[4,48,384]{2,1,0:T(8,128)S(1)}, f32[4,48,384]{2,1,0:T(8,128)S(1)}, u32[]{:S(2)}, u32[]{:S(2)}) collective-permute-start(f32[4,48,384]{2,1,0:T(8,128)S(1)} %get-tuple-element.11), channel_id=1, source_target_pairs={{8,24},{12,28},{9,25},{13,29},{10,26},{14,30},{11,27},{15,31}} | collective-permute-start | bytes 884744 | tf_op jit(solution)/shard_map/ppermute | solution.py:215
  14.5 4.9 %collective-permute-start.8 = (f32[4,48,384]{2,1,0:T(8,128)S(1)}, f32[4,48,384]{2,1,0:T(8,128)S(1)}, u32[]{:S(2)}, u32[]{:S(2)}) collective-permute-start(f32[4,48,384]{2,1,0:T(8,128)S(1)} %collective-permute-done.1.first.step), channel_id=1, source_target_pairs={{0,4},{4,0},{8,12},{12,8},{16,20},{20,16},{24,28},{28,24},{1,5},{5... | collective-permute-start | bytes 884744 | tf_op jit(solution)/shard_map/ppermute | solution.py:196
  14.5 4.9 %collective-permute-start.10 = (f32[4,48,384]{2,1,0:T(8,128)S(1)}, f32[4,48,384]{2,1,0:T(8,128)S(1)}, u32[]{:S(2)}, u32[]{:S(2)}) collective-permute-start(f32[4,48,384]{2,1,0:T(8,128)S(1)} %collective-permute-done.9.skip), channel_id=1, source_target_pairs={{0,4},{4,0},{8,12},{12,8},{16,20},{20,16},{24,28},{28,24},{1,5},{5... | collective-permute-start | bytes 884744 | tf_op jit(solution)/shard_map/ppermute | solution.py:196
  15.0 12.3 %collective-permute-start.5 = (f32[96,384]{1,0:T(8,128)S(1)}, f32[96,384]{1,0:T(8,128)S(1)}, u32[]{:S(2)}, u32[]{:S(2)}) collective-permute-start(f32[96,384]{1,0:T(8,128)S(1)} %get-tuple-element.12.rows), channel_id=1, source_target_pairs={{0,1},{1,0},{2,3},{3,2},{4,5},{5,4},{6,7},{7,6},{8,9},{9,8},{10,11... | collective-permute-start | bytes 442376 | tf_op jit(solution)/shard_map/ppermute | solution.py:209
  16.6 10.7 %collective-permute-start.6 = (f32[96,256]{1,0:T(8,128)S(1)}, f32[96,256]{1,0:T(8,128)S(1)}, u32[]{:S(2)}, u32[]{:S(2)}) collective-permute-start(f32[96,256]{1,0:T(8,128)S(1)} %get-tuple-element.13), channel_id=1, source_target_pairs={{0,2},{1,3},{2,0},{3,1},{4,6},{5,7},{6,4},{7,5},{8,10},{9,11},{10,... | collective-permute-start | bytes 294920 | tf_op jit(solution)/shard_map/ppermute | solution.py:209
  19.2 8.2 %collective-permute-start.7 = (f32[96,256]{1,0:T(8,128)S(1)}, f32[96,256]{1,0:T(8,128)S(1)}, u32[]{:S(2)}, u32[]{:S(2)}) collective-permute-start(f32[96,256]{1,0:T(8,128)S(1)} %get-tuple-element.13), channel_id=1, source_target_pairs={{0,3},{1,2},{2,1},{3,0},{4,7},{5,6},{6,5},{7,4},{8,11},{9,10},{10,... | collective-permute-start | bytes 294920 | tf_op jit(solution)/shard_map/ppermute | solution.py:209
  27.7 15.3 %collective-permute-start.11 = (f32[384,384]{1,0:T(8,128)S(1)}, f32[384,384]{1,0:T(8,128)S(1)}, u32[]{:S(2)}, u32[]{:S(2)}) collective-permute-start(f32[384,384]{1,0:T(8,128)S(1)} %shard_map.32.one), channel_id=1, source_target_pairs={{0,4},{4,0},{8,12},{12,8},{16,20},{20,16},{24,28},{28,24},{1,5},{5... | collective-permute-start | bytes 1769480 | tf_op jit(solution)/shard_map/ppermute | solution.py:196
  27.8 13.4 %collective-permute-start.2 = (f32[4,48,384]{2,1,0:T(8,128)S(1)}, f32[4,48,384]{2,1,0:T(8,128)S(1)}, u32[]{:S(2)}, u32[]{:S(2)}) collective-permute-start(f32[4,48,384]{2,1,0:T(8,128)S(1)} %get-tuple-element.11), channel_id=1, source_target_pairs={{0,16},{4,20},{1,17},{5,21},{2,18},{6,22},{3,19},{7,23}} | collective-permute-start | bytes 884744 | tf_op jit(solution)/shard_map/ppermute | solution.py:215
  34.3 8.6 %collective-permute-start.3 = (f32[4,48,384]{2,1,0:T(8,128)S(1)}, f32[4,48,384]{2,1,0:T(8,128)S(1)}, u32[]{:S(2)}, u32[]{:S(2)}) collective-permute-start(f32[4,48,384]{2,1,0:T(8,128)S(1)} %get-tuple-element.11), channel_id=1, source_target_pairs={{0,24},{4,28},{1,25},{5,29},{2,26},{6,30},{3,27},{7,31}} | collective-permute-start | bytes 884744 | tf_op jit(solution)/shard_map/ppermute | solution.py:215
  42.9 1.6 %collective-permute-start.4 = (f32[4,48,384]{2,1,0:T(8,128)S(1)}, f32[4,48,384]{2,1,0:T(8,128)S(1)}, u32[]{:S(2)}, u32[]{:S(2)}) collective-permute-start(f32[4,48,384]{2,1,0:T(8,128)S(1)} %shard_map.30.mine), channel_id=1, source_target_pairs={{0,4},{4,0},{8,12},{12,8},{16,20},{20,16},{24,28},{28,24},{1,5},{5... | collective-permute-start | bytes 884744 | tf_op jit(solution)/shard_map/ppermute | solution.py:196
  44.6 6.7 %collective-permute-start.12 = (f32[48,384]{1,0:T(8,128)S(1)}, f32[48,384]{1,0:T(8,128)S(1)}, u32[]{:S(2)}, u32[]{:S(2)}) collective-permute-start(f32[48,384]{1,0:T(8,128)S(1)} %get-tuple-element.15), channel_id=1, source_target_pairs={{0,24},{4,28},{8,16},{12,20},{16,8},{20,12},{24,0},{28,4},{1,25},{... | collective-permute-start | bytes 221192 | tf_op jit(solution)/shard_map/ppermute | solution.py:230
  48.6 4.4 %collective-permute-start.13 = (f32[48,384]{1,0:T(8,128)S(1)}, f32[48,384]{1,0:T(8,128)S(1)}, u32[]{:S(2)}, u32[]{:S(2)}) collective-permute-start(f32[48,384]{1,0:T(8,128)S(1)} %get-tuple-element.17), channel_id=1, source_target_pairs={{0,16},{4,20},{8,24},{12,28},{16,0},{20,4},{24,8},{28,12},{1,17},{... | collective-permute-start | bytes 221192 | tf_op jit(solution)/shard_map/ppermute | solution.py:230
  48.6 4.4 %collective-permute-start.14 = (f32[48,384]{1,0:T(8,128)S(1)}, f32[48,384]{1,0:T(8,128)S(1)}, u32[]{:S(2)}, u32[]{:S(2)}) collective-permute-start(f32[48,384]{1,0:T(8,128)S(1)} %get-tuple-element.16), channel_id=1, source_target_pairs={{0,8},{4,12},{8,0},{12,4},{16,24},{20,28},{24,16},{28,20},{1,9},{5... | collective-permute-start | bytes 221192 | tf_op jit(solution)/shard_map/ppermute | solution.py:230

commit v6 on v5

--- a/solution.py
+++ b/solution.py
@@ -184,6 +184,12 @@
         fill(whole, core, mine, theirs)
         right = parts(whole[...].reshape(order_dim, order_dim))
         out[...] = mul(parts(left[...].reshape(chips * rows, order_dim)), right, 1).reshape(out.shape)
+
+
+def sum_kernel(terms, *refs):
+    received, out = refs[:-1], refs[-1]
+    chip = lax.axis_index("tm") // 2
+    out[...] = terms[chip] + (received[0][...] + (received[1][...] + received[2][...]))
 
 
 def body(propagators, perturbation):
@@ -224,10 +230,11 @@
     theirs = swap(mine)
     (left,) = call(left_kernel, [half_shape], [mine, one, two], [own.shape], 2 * cube)
     (terms,) = call(right_kernel, [half_shape], [mine, theirs, left], [whole_shape], 2 * cube)
-    out = lax.dynamic_index_in_dim(terms, chip, 0, False)
+    received = []
     for way in (3, 2, 1):
         block = lax.dynamic_index_in_dim(terms, chip ^ way, 0, False)
-        out = out + lax.ppermute(block, "tm", [(i, i ^ (2 * way)) for i in range(devices)])
+        received.append(lax.ppermute(block, "tm", [(i, i ^ (2 * way)) for i in range(devices)]))
+    (out,) = call(sum_kernel, [(out_rows, order_dim)], [terms] + received)
     return out
 
 

time: 53.9 us -> 53.9 us (level)
  Pallas kernels: 1.15 us -> 1.8 us
  other arithmetic: 0.65 us -> 0 us
    add x1 -> x0, other arithmetic: 0.65 us -> none  [body(): out + lax.ppermute(block, 'tm', [(i, i ^ 2 * way) for i in range(devices)])]
    pallas_call x7 -> x8, Pallas kernels: 1.15 us -> 1.8 us  [call(): pl.pallas_call(kernel, out_shape=outs, in_specs=[VMEM] * len(operands), o...]
where the time goes in v6:
time: 53.9 us; the launch traced here: 53.6 us
  waiting for transfers between devices  26.1 us (48%)
  starting transfers between devices  23.7 us (44%)
  local copies, waits for them, and re-layouts  2 us (4%)
  Pallas kernels  1.8 us (3%)
    ppermute x4, starting transfers between devices, body(): lax.ppermute(half, 'tm', [(2 * i + c, 2 * j + c) for i, j in links for c...  13.4 us
    ppermute x4, waiting for transfers between devices, body(): lax.ppermute(half, 'tm', [(2 * i + c, 2 * j + c) for i, j in links for c...  12.9 us
    ppermute x3, waiting for transfers between devices, body(): lax.ppermute(sent, 'group', [(i, i ^ way) for i in range(planes)])  7.92 us
    ppermute x3, starting transfers between devices, body(): lax.ppermute(block, 'tm', [(i, i ^ 2 * way) for i in range(devices)])  4.68 us
    ppermute x3, starting transfers between devices, body(): lax.ppermute(sent, 'group', [(i, i ^ way) for i in range(planes)])  4.39 us
    ppermute x3, waiting for transfers between devices, body(): lax.ppermute(block, 'tm', [(i, i ^ 2 * way) for i in range(devices)])  3.71 us
    unnamed x4, local copies, waits for them, and re-layouts  1.97 us
    pallas_call x8, Pallas kernels, call(): pl.pallas_call(kernel, out_shape=outs, in_specs=[VMEM] * len(operands), o...  1.8 us
  transfers between devices with their start and end apart: 15, of which 7 were waited for; matrix products, arithmetic and copies ran while one was open for 0% of the time, Pallas kernels for 0%

profile of v6, /device:TPU:0, one launch (start us, length us, event | category | flops | bytes accessed | tf_op | source)
XLA Modules:
  0.0 53.6 jit_solution(10807743012027606507)
XLA Ops:
  0.0 0.5 collective-permute-start
  0.5 0.0 copy-start
  0.5 1.1 %copy-done = f32[1,384,384]{2,1,0:T(8,128)S(1)} copy-done((f32[1,384,384]{2,1,0:T(8,128)S(1)}, f32[1,384,384]{2,1,0:T(8,128)}, u32[]{:S(2)}) %copy-start) | copy-done | bytes 589848
  1.6 0.0 copy-start.1
  1.6 0.9 %copy-done.1 = f32[1,96,384]{2,1,0:T(8,128)S(1)} copy-done((f32[1,96,384]{2,1,0:T(8,128)S(1)}, f32[1,96,384]{2,1,0:T(8,128)}, u32[]{:S(2)}) %copy-start.1) | copy-done | bytes 147480
  2.5 0.1 shard_map.28
  2.5 0.0 collective-permute-done.other.even
  2.5 0.7 %shard_map.29 = (f32[4,48,384]{2,1,0:T(8,128)S(1)}, f32[384,384]{1,0:T(8,128)S(1)}) custom-call(f32[384,384]{1,0:T(8,128)S(1)} %get-tuple-element.10.own, f32[384,384]{1,0:T(8,128)S(1)} %collective-permute-done.other.even), custom_call_target="tpu_custom_call" | custom-call | flops 226492416 | tf_op jit(solution)/shard_map/pallas_call | solution.py:31
  3.2 4.5 %collective-permute-start.1 = (f32[4,48,384]{2,1,0:T(8,128)S(1)}, f32[4,48,384]{2,1,0:T(8,128)S(1)}, u32[]{:S(2)}, u32[]{:S(2)}) collective-permute-start(f32[4,48,384]{2,1,0:T(8,128)S(1)} %get-tuple-element.11), channel_id=1, source_target_pairs={{0,8},{4,12},{8,16},{12,20},{16,24},{20,28},{1,9},{5,13},{9,17},{1... | collective-permute-start | bytes 884744 | tf_op jit(solution)/shard_map/ppermute | solution.py:221
  7.8 0.7 %collective-permute-start.9 = (f32[4,48,384]{2,1,0:T(8,128)S(1)}, f32[4,48,384]{2,1,0:T(8,128)S(1)}, u32[]{:S(2)}, u32[]{:S(2)}) collective-permute-start(f32[4,48,384]{2,1,0:T(8,128)S(1)} %get-tuple-element.11), channel_id=1, source_target_pairs={{8,24},{12,28},{9,25},{13,29},{10,26},{14,30},{11,27},{15,31}} | collective-permute-start | bytes 884744 | tf_op jit(solution)/shard_map/ppermute | solution.py:221
  8.5 6.1 %collective-permute-done.1.first.step = f32[4,48,384]{2,1,0:T(8,128)S(1)} collective-permute-done((f32[4,48,384]{2,1,0:T(8,128)S(1)}, f32[4,48,384]{2,1,0:T(8,128)S(1)}, u32[]{:S(2)}, u32[]{:S(2)}) %collective-permute-start.1) | collective-permute-done | bytes 294944 | tf_op jit(solution)/shard_map/ppermute | solution.py:221
  14.5 0.0 collective-permute-start.8
  14.5 0.0 collective-permute-done.9.skip
  14.5 0.5 collective-permute-start.10
  15.0 1.6 %collective-permute-start.5 = (f32[96,384]{1,0:T(8,128)S(1)}, f32[96,384]{1,0:T(8,128)S(1)}, u32[]{:S(2)}, u32[]{:S(2)}) collective-permute-start(f32[96,384]{1,0:T(8,128)S(1)} %get-tuple-element.12.rows), channel_id=1, source_target_pairs={{0,1},{1,0},{2,3},{3,2},{4,5},{5,4},{6,7},{7,6},{8,9},{9,8},{10,11... | collective-permute-start | bytes 442376 | tf_op jit(solution)/shard_map/ppermute | solution.py:215
  16.6 2.6 %collective-permute-start.6 = (f32[96,256]{1,0:T(8,128)S(1)}, f32[96,256]{1,0:T(8,128)S(1)}, u32[]{:S(2)}, u32[]{:S(2)}) collective-permute-start(f32[96,256]{1,0:T(8,128)S(1)} %get-tuple-element.13), channel_id=1, source_target_pairs={{0,2},{1,3},{2,0},{3,1},{4,6},{5,7},{6,4},{7,5},{8,10},{9,11},{10,... | collective-permute-start | bytes 294920 | tf_op jit(solution)/shard_map/ppermute | solution.py:215
  19.2 0.2 collective-permute-start.7
  19.4 0.0 collective-permute-done.8.step_other
  19.4 0.0 collective-permute-done.10.skip_other
  19.4 7.9 %collective-permute-done.6.skip = f32[96,256]{1,0:T(8,128)S(1)} collective-permute-done((f32[96,256]{1,0:T(8,128)S(1)}, f32[96,256]{1,0:T(8,128)S(1)}, u32[]{:S(2)}, u32[]{:S(2)}) %collective-permute-start.6) | collective-permute-done | bytes 98336 | tf_op jit(solution)/shard_map/ppermute | solution.py:215
  27.4 0.0 collective-permute-done.7.cross
  27.4 0.0 collective-permute-done.5.beside
  27.4 0.3 shard_map.32.one
  27.7 0.1 collective-permute-start.11
  27.8 6.5 %collective-permute-start.2 = (f32[4,48,384]{2,1,0:T(8,128)S(1)}, f32[4,48,384]{2,1,0:T(8,128)S(1)}, u32[]{:S(2)}, u32[]{:S(2)}) collective-permute-start(f32[4,48,384]{2,1,0:T(8,128)S(1)} %get-tuple-element.11), channel_id=1, source_target_pairs={{0,16},{4,20},{1,17},{5,21},{2,18},{6,22},{3,19},{7,23}} | collective-permute-start | bytes 884744 | tf_op jit(solution)/shard_map/ppermute | solution.py:221
  34.3 1.8 %collective-permute-start.3 = (f32[4,48,384]{2,1,0:T(8,128)S(1)}, f32[4,48,384]{2,1,0:T(8,128)S(1)}, u32[]{:S(2)}, u32[]{:S(2)}) collective-permute-start(f32[4,48,384]{2,1,0:T(8,128)S(1)} %get-tuple-element.11), channel_id=1, source_target_pairs={{0,24},{4,28},{1,25},{5,29},{2,26},{6,30},{3,27},{7,31}} | collective-permute-start | bytes 884744 | tf_op jit(solution)/shard_map/ppermute | solution.py:221
  36.1 5.1 %collective-permute-done.2.second = f32[4,48,384]{2,1,0:T(8,128)S(1)} collective-permute-done((f32[4,48,384]{2,1,0:T(8,128)S(1)}, f32[4,48,384]{2,1,0:T(8,128)S(1)}, u32[]{:S(2)}, u32[]{:S(2)}) %collective-permute-start.2) | collective-permute-done | bytes 294944 | tf_op jit(solution)/shard_map/ppermute | solution.py:221
  41.2 1.8 %collective-permute-done.3.third = f32[4,48,384]{2,1,0:T(8,128)S(1)} collective-permute-done((f32[4,48,384]{2,1,0:T(8,128)S(1)}, f32[4,48,384]{2,1,0:T(8,128)S(1)}, u32[]{:S(2)}, u32[]{:S(2)}) %collective-permute-start.3) | collective-permute-done | bytes 294944 | tf_op jit(solution)/shard_map/ppermute | solution.py:221
  42.9 0.0 collective-permute-start.4
  43.0 0.0 collective-permute-done.11.two
  43.0 0.1 shard_map.33.left
  43.0 1.5 %collective-permute-done.4.theirs = f32[4,48,384]{2,1,0:T(8,128)S(1)} collective-permute-done((f32[4,48,384]{2,1,0:T(8,128)S(1)}, f32[4,48,384]{2,1,0:T(8,128)S(1)}, u32[]{:S(2)}, u32[]{:S(2)}) %collective-permute-start.4) | collective-permute-done | bytes 294944 | tf_op jit(solution)/shard_map/ppermute | solution.py:202
  44.6 4.0 %collective-permute-start.12 = (f32[48,384]{1,0:T(8,128)S(1)}, f32[48,384]{1,0:T(8,128)S(1)}, u32[]{:S(2)}, u32[]{:S(2)}) collective-permute-start(f32[48,384]{1,0:T(8,128)S(1)} %get-tuple-element.17), channel_id=1, source_target_pairs={{0,24},{4,28},{8,16},{12,20},{16,8},{20,12},{24,0},{28,4},{1,25},{... | collective-permute-start | bytes 221192 | tf_op jit(solution)/shard_map/ppermute | solution.py:236
  48.6 0.0 collective-permute-start.13
  48.6 0.6 %collective-permute-start.14 = (f32[48,384]{1,0:T(8,128)S(1)}, f32[48,384]{1,0:T(8,128)S(1)}, u32[]{:S(2)}, u32[]{:S(2)}) collective-permute-start(f32[48,384]{1,0:T(8,128)S(1)} %get-tuple-element.15), channel_id=1, source_target_pairs={{0,8},{4,12},{8,0},{12,4},{16,24},{20,28},{24,16},{28,20},{1,9},{5... | collective-permute-start | bytes 221192 | tf_op jit(solution)/shard_map/ppermute | solution.py:236
  49.3 2.0 %collective-permute-done.12.refs_0_ = f32[48,384]{1,0:T(8,128)S(1)} collective-permute-done((f32[48,384]{1,0:T(8,128)S(1)}, f32[48,384]{1,0:T(8,128)S(1)}, u32[]{:S(2)}, u32[]{:S(2)}) %collective-permute-start.12) | collective-permute-done | bytes 73760 | tf_op jit(solution)/shard_map/ppermute | solution.py:236
  51.3 1.7 %collective-permute-done.13.refs_1_ = f32[48,384]{1,0:T(8,128)S(1)} collective-permute-done((f32[48,384]{1,0:T(8,128)S(1)}, f32[48,384]{1,0:T(8,128)S(1)}, u32[]{:S(2)}, u32[]{:S(2)}) %collective-permute-start.13) | collective-permute-done | bytes 73760 | tf_op jit(solution)/shard_map/ppermute | solution.py:236
  53.0 0.0 collective-permute-done.14.refs_2_
  53.0 0.7 %shard_map.35 = f32[48,384]{1,0:T(8,128)} custom-call(f32[4,48,384]{2,1,0:T(8,128)S(1)} %shard_map.34.terms, f32[48,384]{1,0:T(8,128)S(1)} %collective-permute-done.12.refs_0_, f32[48,384]{1,0:T(8,128)S(1)} %collective-permute-done.13.refs_1_, f32[48,384]{1,0:T(8,128)S(1)} %collective-permute-done.14.refs_2_), custom_call_target="tpu_custom_call" | custom-call | tf_op jit(solution)/shard_map/pallas_call | solution.py:31
  (4 shorter events, 0.0 us)
Async XLA Ops:
  0.0 2.5 %collective-permute-start = (f32[384,384]{1,0:T(8,128)}, f32[384,384]{1,0:T(8,128)S(1)}, u32[]{:S(2)}, u32[]{:S(2)}) collective-permute-start(f32[384,384]{1,0:T(8,128)} %bitcast.8), channel_id=1, source_target_pairs={{0,4},{4,0},{8,12},{12,8},{16,20},{20,16},{24,28},{28,24},{1,5},{5... | collective-permute-start | bytes 1769480 | tf_op jit(solution)/shard_map/ppermute | solution.py:202
  0.5 1.1 %copy-start = (f32[1,384,384]{2,1,0:T(8,128)S(1)}, f32[1,384,384]{2,1,0:T(8,128)}, u32[]{:S(2)}) copy-start(f32[1,384,384]{2,1,0:T(8,128)} %param.2) | copy-start | bytes 1769476
  1.6 0.9 %copy-start.1 = (f32[1,96,384]{2,1,0:T(8,128)S(1)}, f32[1,96,384]{2,1,0:T(8,128)}, u32[]{:S(2)}) copy-start(f32[1,96,384]{2,1,0:T(8,128)} %param.3) | copy-start | bytes 442372
  3.2 11.3 %collective-permute-start.1 = (f32[4,48,384]{2,1,0:T(8,128)S(1)}, f32[4,48,384]{2,1,0:T(8,128)S(1)}, u32[]{:S(2)}, u32[]{:S(2)}) collective-permute-start(f32[4,48,384]{2,1,0:T(8,128)S(1)} %get-tuple-element.11), channel_id=1, source_target_pairs={{0,8},{4,12},{8,16},{12,20},{16,24},{20,28},{1,9},{5,13},{9,17},{1... | collective-permute-start | bytes 884744 | tf_op jit(solution)/shard_map/ppermute | solution.py:221
  7.8 6.8 %collective-permute-start.9 = (f32[4,48,384]{2,1,0:T(8,128)S(1)}, f32[4,48,384]{2,1,0:T(8,128)S(1)}, u32[]{:S(2)}, u32[]{:S(2)}) collective-permute-start(f32[4,48,384]{2,1,0:T(8,128)S(1)} %get-tuple-element.11), channel_id=1, source_target_pairs={{8,24},{12,28},{9,25},{13,29},{10,26},{14,30},{11,27},{15,31}} | collective-permute-start | bytes 884744 | tf_op jit(solution)/shard_map/ppermute | solution.py:221
  14.5 4.9 %collective-permute-start.8 = (f32[4,48,384]{2,1,0:T(8,128)S(1)}, f32[4,48,384]{2,1,0:T(8,128)S(1)}, u32[]{:S(2)}, u32[]{:S(2)}) collective-permute-start(f32[4,48,384]{2,1,0:T(8,128)S(1)} %collective-permute-done.1.first.step), channel_id=1, source_target_pairs={{0,4},{4,0},{8,12},{12,8},{16,20},{20,16},{24,28},{28,24},{1,5},{5... | collective-permute-start | bytes 884744 | tf_op jit(solution)/shard_map/ppermute | solution.py:202
  14.5 4.9 %collective-permute-start.10 = (f32[4,48,384]{2,1,0:T(8,128)S(1)}, f32[4,48,384]{2,1,0:T(8,128)S(1)}, u32[]{:S(2)}, u32[]{:S(2)}) collective-permute-start(f32[4,48,384]{2,1,0:T(8,128)S(1)} %collective-permute-done.9.skip), channel_id=1, source_target_pairs={{0,4},{4,0},{8,12},{12,8},{16,20},{20,16},{24,28},{28,24},{1,5},{5... | collective-permute-start | bytes 884744 | tf_op jit(solution)/shard_map/ppermute | solution.py:202
  15.0 12.3 %collective-permute-start.5 = (f32[96,384]{1,0:T(8,128)S(1)}, f32[96,384]{1,0:T(8,128)S(1)}, u32[]{:S(2)}, u32[]{:S(2)}) collective-permute-start(f32[96,384]{1,0:T(8,128)S(1)} %get-tuple-element.12.rows), channel_id=1, source_target_pairs={{0,1},{1,0},{2,3},{3,2},{4,5},{5,4},{6,7},{7,6},{8,9},{9,8},{10,11... | collective-permute-start | bytes 442376 | tf_op jit(solution)/shard_map/ppermute | solution.py:215
  16.6 10.7 %collective-permute-start.6 = (f32[96,256]{1,0:T(8,128)S(1)}, f32[96,256]{1,0:T(8,128)S(1)}, u32[]{:S(2)}, u32[]{:S(2)}) collective-permute-start(f32[96,256]{1,0:T(8,128)S(1)} %get-tuple-element.13), channel_id=1, source_target_pairs={{0,2},{1,3},{2,0},{3,1},{4,6},{5,7},{6,4},{7,5},{8,10},{9,11},{10,... | collective-permute-start | bytes 294920 | tf_op jit(solution)/shard_map/ppermute | solution.py:215
  19.2 8.2 %collective-permute-start.7 = (f32[96,256]{1,0:T(8,128)S(1)}, f32[96,256]{1,0:T(8,128)S(1)}, u32[]{:S(2)}, u32[]{:S(2)}) collective-permute-start(f32[96,256]{1,0:T(8,128)S(1)} %get-tuple-element.13), channel_id=1, source_target_pairs={{0,3},{1,2},{2,1},{3,0},{4,7},{5,6},{6,5},{7,4},{8,11},{9,10},{10,... | collective-permute-start | bytes 294920 | tf_op jit(solution)/shard_map/ppermute | solution.py:215
  27.7 15.3 %collective-permute-start.11 = (f32[384,384]{1,0:T(8,128)S(1)}, f32[384,384]{1,0:T(8,128)S(1)}, u32[]{:S(2)}, u32[]{:S(2)}) collective-permute-start(f32[384,384]{1,0:T(8,128)S(1)} %shard_map.32.one), channel_id=1, source_target_pairs={{0,4},{4,0},{8,12},{12,8},{16,20},{20,16},{24,28},{28,24},{1,5},{5... | collective-permute-start | bytes 1769480 | tf_op jit(solution)/shard_map/ppermute | solution.py:202
  27.8 13.4 %collective-permute-start.2 = (f32[4,48,384]{2,1,0:T(8,128)S(1)}, f32[4,48,384]{2,1,0:T(8,128)S(1)}, u32[]{:S(2)}, u32[]{:S(2)}) collective-permute-start(f32[4,48,384]{2,1,0:T(8,128)S(1)} %get-tuple-element.11), channel_id=1, source_target_pairs={{0,16},{4,20},{1,17},{5,21},{2,18},{6,22},{3,19},{7,23}} | collective-permute-start | bytes 884744 | tf_op jit(solution)/shard_map/ppermute | solution.py:221
  34.3 8.6 %collective-permute-start.3 = (f32[4,48,384]{2,1,0:T(8,128)S(1)}, f32[4,48,384]{2,1,0:T(8,128)S(1)}, u32[]{:S(2)}, u32[]{:S(2)}) collective-permute-start(f32[4,48,384]{2,1,0:T(8,128)S(1)} %get-tuple-element.11), channel_id=1, source_target_pairs={{0,24},{4,28},{1,25},{5,29},{2,26},{6,30},{3,27},{7,31}} | collective-permute-start | bytes 884744 | tf_op jit(solution)/shard_map/ppermute | solution.py:221
  42.9 1.6 %collective-permute-start.4 = (f32[4,48,384]{2,1,0:T(8,128)S(1)}, f32[4,48,384]{2,1,0:T(8,128)S(1)}, u32[]{:S(2)}, u32[]{:S(2)}) collective-permute-start(f32[4,48,384]{2,1,0:T(8,128)S(1)} %shard_map.30.mine), channel_id=1, source_target_pairs={{0,4},{4,0},{8,12},{12,8},{16,20},{20,16},{24,28},{28,24},{1,5},{5... | collective-permute-start | bytes 884744 | tf_op jit(solution)/shard_map/ppermute | solution.py:202
  44.6 6.7 %collective-permute-start.12 = (f32[48,384]{1,0:T(8,128)S(1)}, f32[48,384]{1,0:T(8,128)S(1)}, u32[]{:S(2)}, u32[]{:S(2)}) collective-permute-start(f32[48,384]{1,0:T(8,128)S(1)} %get-tuple-element.17), channel_id=1, source_target_pairs={{0,24},{4,28},{8,16},{12,20},{16,8},{20,12},{24,0},{28,4},{1,25},{... | collective-permute-start | bytes 221192 | tf_op jit(solution)/shard_map/ppermute | solution.py:236
  48.6 4.4 %collective-permute-start.13 = (f32[48,384]{1,0:T(8,128)S(1)}, f32[48,384]{1,0:T(8,128)S(1)}, u32[]{:S(2)}, u32[]{:S(2)}) collective-permute-start(f32[48,384]{1,0:T(8,128)S(1)} %get-tuple-element.16), channel_id=1, source_target_pairs={{0,16},{4,20},{8,24},{12,28},{16,0},{20,4},{24,8},{28,12},{1,17},{... | collective-permute-start | bytes 221192 | tf_op jit(solution)/shard_map/ppermute | solution.py:236
  48.6 4.4 %collective-permute-start.14 = (f32[48,384]{1,0:T(8,128)S(1)}, f32[48,384]{1,0:T(8,128)S(1)}, u32[]{:S(2)}, u32[]{:S(2)}) collective-permute-start(f32[48,384]{1,0:T(8,128)S(1)} %get-tuple-element.15), channel_id=1, source_target_pairs={{0,8},{4,12},{8,0},{12,4},{16,24},{20,28},{24,16},{28,20},{1,9},{5... | collective-permute-start | bytes 221192 | tf_op jit(solution)/shard_map/ppermute | solution.py:236
